TPU v7x, 256 devices: a whole 4x4x8 slice. The times are simulated.
256 devices in a mesh: ctx: 32 (over x_hi, z, core), head: 8 (over x_lo, y).
Axes of the slice: x: 4 (x_hi: 2, x_lo: 2; x = x_hi * 2 + x_lo), y: 4, z: 8, core: 2. Of those that a mesh axis runs over, the one named last changes fastest.
Arguments:
- queries: bfloat16 [2, 4096, 8192], P(None, ('ctx', 'head')), as said below
- keys: bfloat16 [2, 4096, 1024], P(None, ('ctx', 'head')), as said below
- values: bfloat16 [2, 4096, 1024], P(None, ('ctx', 'head')), may hold values from -6 to 6
- outputs: bfloat16 [2, 4096, 8192], P(None, ('ctx', 'head')), may hold values from -4 to 4
- cotangent: bfloat16 [2, 4096, 8192], P(None, ('ctx', 'head')), may hold values from -4 to 4
- lengths: int32 [256], replicated, may hold values from 1 to 32, 4096 in all
Outputs:
- grad_queries: bfloat16 [2, 4096, 8192], P(None, ('ctx', 'head'))
- grad_keys: float32 [2, 4096, 1024], P(None, ('ctx', 'head'))
- grad_values: float32 [2, 4096, 1024], P(None, ('ctx', 'head'))
Inputs may be any that keep to these rules, and one draw needn't show every extreme that they name: `lengths`: they sum to 4096, and one of them is exactly 32. `queries`: real-valued entries. `keys`: real-valued entries.
All inputs are finite; a program needn't handle non-finite values.
Results may differ from a plain program's by a relative error of at most 0.0025.
The roundings to bfloat16 on the way count: a program that leaves them out, or rounds other values in their place, can miss the bound.
Values may be sent and summed in bfloat16 or wider, within the bound.
A program may use at most 64 MiB of HBM per device.

v0:
```python
import math

import jax
import jax.numpy as jnp
from jax import lax
from jax.sharding import PartitionSpec as P

HD = 128


NEG_FILL = -1e30


def passed_along(value, axis, steps):
    count = lax.axis_size(axis)
    initial, last = (max(0, -steps), min(count, count - steps))
    return lax.ppermute(value, axis, [(source, source + steps) for source in range(initial, last)])


def question_segments(lengths, offsets):
    starts = jnp.cumsum(lengths) - lengths
    matched = (starts[None, :] <= offsets[:, None]).astype(jnp.int32)
    return jnp.sum(matched, axis=1)


def allowed(query_pos, query_seg, key_pos, key_seg):
    same_doc = (key_seg[None, :] == 0) | (key_seg[None, :] == query_seg[:, None])
    return (key_pos[None, :] <= query_pos[:, None]) & same_doc


def split_heads(matrix, kv_local):
    row_count = matrix.shape[0]
    return matrix.reshape(row_count, kv_local, matrix.shape[1] // (kv_local * HD), HD)


def row_products(out_rows, cot_rows, kv_local):
    cot_four = split_heads(cot_rows, kv_local)
    out_four = split_heads(out_rows, kv_local)
    products = jnp.sum(cot_four.astype(jnp.float32) * out_four.astype(jnp.float32), axis=-1)
    return jnp.transpose(products, (1, 2, 0))


def make_group(query_rows, cot_rows, products, positions, segments, kv_local):
    return {
        "query": split_heads(query_rows, kv_local),
        "cot": split_heads(cot_rows, kv_local),
        "pos": positions,
        "seg": segments,
        "delta": products,
    }


def block_scores(query_four, key_block, score_scale):
    key_three = key_block.reshape(key_block.shape[0], query_four.shape[1], HD)
    return (
        jnp.einsum("rkgd,skd->kgrs", query_four, key_three, preferred_element_type=jnp.float32)
        * score_scale
    )


def stats_update(state_now, query_set, key_block, key_pos, key_seg, score_scale):
    run_max, run_sum = state_now
    scores = block_scores(query_set["query"], key_block, score_scale)
    visible = allowed(query_set["pos"], query_set["seg"], key_pos, key_seg)[None, None]
    new_max = jnp.maximum(run_max, jnp.max(jnp.where(visible, scores, NEG_FILL), axis=-1))
    weights = jnp.where(visible, jnp.exp(scores - new_max[..., None]), 0.0)
    return (new_max, run_sum * jnp.exp(run_max - new_max) + jnp.sum(weights, axis=-1))


def block_backward(query_set, key_block, value_block, key_pos, key_seg, score_scale):
    query_four = query_set["query"]
    cot_four = query_set["cot"]
    kv_local = query_four.shape[1]
    key_three = key_block.reshape(key_block.shape[0], kv_local, HD)
    value_three = value_block.reshape(value_block.shape[0], kv_local, HD)
    scores = block_scores(query_four, key_block, score_scale)
    visible = allowed(query_set["pos"], query_set["seg"], key_pos, key_seg)[None, None]
    attn_prob = jnp.where(visible, jnp.exp(scores - query_set["log_sum"][..., None]), 0.0)
    prob_low = attn_prob.astype(jnp.bfloat16)
    d_prob = jnp.einsum("rkgd,skd->kgrs", cot_four, value_three, preferred_element_type=jnp.float32)
    dscore = (attn_prob * (d_prob - query_set["delta"][..., None])).astype(jnp.bfloat16)
    dquery = (
        jnp.einsum("kgrs,skd->rkgd", dscore, key_three, preferred_element_type=jnp.float32)
        * score_scale
    )
    d_key = (
        jnp.einsum("kgrs,rkgd->skd", dscore, query_four, preferred_element_type=jnp.float32)
        * score_scale
    )
    dvalue = jnp.einsum("kgrs,rkgd->skd", prob_low, cot_four, preferred_element_type=jnp.float32)
    feat_width = key_block.shape[1]
    return (dquery, d_key.reshape(-1, feat_width), dvalue.reshape(-1, feat_width))


def block_limit(query_set, block_len, total_blocks):
    return jnp.minimum(jnp.max(query_set["pos"]) // block_len + 1, total_blocks)


def with_log_sum(query_set, doc_keys, block_len, total_blocks, extra_keys, score_scale):
    query_four = query_set["query"]
    stat_shape = (query_four.shape[1], query_four.shape[2], query_four.shape[0])
    start_state = (jnp.full(stat_shape, NEG_FILL, jnp.float32), jnp.zeros(stat_shape, jnp.float32))

    def with_visit(block_no, state_now):
        first_row = block_no * block_len
        key_block = lax.dynamic_slice_in_dim(doc_keys, first_row, block_len, 0)
        key_pos = first_row + jnp.arange(block_len, dtype=jnp.int32)
        key_seg = jnp.zeros((block_len,), jnp.int32)
        return stats_update(state_now, query_set, key_block, key_pos, key_seg, score_scale)

    state_now = lax.fori_loop(
        0, block_limit(query_set, block_len, total_blocks), with_visit, start_state
    )
    if extra_keys is not None:
        state_now = stats_update(
            state_now, query_set, extra_keys[0], extra_keys[2], extra_keys[3], score_scale
        )
    return dict(query_set, log_sum=state_now[0] + jnp.log(state_now[1]))


def run_backward(
    query_set, doc_keys, doc_values, block_len, total_blocks, extra_keys, score_scale, doc_buffers
):
    grad_start = jnp.zeros(query_set["query"].shape, jnp.float32)

    def run_visit(block_no, state_now):
        first_row = block_no * block_len
        key_block = lax.dynamic_slice_in_dim(doc_keys, first_row, block_len, 0)
        value_block = lax.dynamic_slice_in_dim(doc_values, first_row, block_len, 0)
        key_pos = first_row + jnp.arange(block_len, dtype=jnp.int32)
        key_seg = jnp.zeros((block_len,), jnp.int32)
        dquery, d_key, dvalue = block_backward(
            query_set, key_block, value_block, key_pos, key_seg, score_scale
        )
        acc_query, acc_key, acc_value = state_now
        acc_key = lax.dynamic_update_slice_in_dim(
            acc_key,
            lax.dynamic_slice_in_dim(acc_key, first_row, block_len, 0) + d_key,
            first_row,
            0,
        )
        acc_value = lax.dynamic_update_slice_in_dim(
            acc_value,
            lax.dynamic_slice_in_dim(acc_value, first_row, block_len, 0) + dvalue,
            first_row,
            0,
        )
        return (acc_query + dquery, acc_key, acc_value)

    limit = block_limit(query_set, block_len, total_blocks)
    grad_query, key_acc, value_acc = lax.fori_loop(
        0, limit, run_visit, (grad_start, doc_buffers[0], doc_buffers[1])
    )
    doc_buffers = (key_acc, value_acc)
    extra_grads = None
    if extra_keys is not None:
        dquery, d_key, dvalue = block_backward(
            query_set, extra_keys[0], extra_keys[1], extra_keys[2], extra_keys[3], score_scale
        )
        grad_query = grad_query + dquery
        extra_grads = (d_key, dvalue)
    return (grad_query, doc_buffers, extra_grads)


def shards(queries, keys, values, outputs, cotangent, lengths):
    head_q, head_o, head_c, head_k, head_v = (
        lax.all_to_all(queries, "head", split_axis=2, concat_axis=1, tiled=True),
        lax.all_to_all(outputs, "head", split_axis=2, concat_axis=1, tiled=True),
        lax.all_to_all(cotangent, "head", split_axis=2, concat_axis=1, tiled=True),
        lax.all_to_all(keys, "head", split_axis=2, concat_axis=1, tiled=True),
        lax.all_to_all(values, "head", split_axis=2, concat_axis=1, tiled=True),
    )
    stretch_len = head_q.shape[1]
    half_len = stretch_len // 2
    kv_local = head_k.shape[2] // HD
    feat_width = head_k.shape[2]
    score_scale = HD ** (-0.5)
    ctx_pos = lax.axis_index("ctx")
    ctx_count = lax.axis_size("ctx")
    doc_len = stretch_len * ctx_count
    block_len = math.gcd(512, doc_len)
    total_blocks = doc_len // block_len
    doc_keys, doc_values = (
        lax.all_gather(head_k[0], "ctx", axis=0, tiled=True),
        lax.all_gather(head_v[0], "ctx", axis=0, tiled=True),
    )
    prev_keys, prev_values = passed_along((head_k[1], head_v[1]), "ctx", 1)
    local_rows = jnp.arange(stretch_len, dtype=jnp.int32)
    own_offsets = ctx_pos * stretch_len + local_rows
    prev_offsets = own_offsets - stretch_len
    own_seg = question_segments(lengths, own_offsets)
    prev_seg = jnp.where(ctx_pos > 0, question_segments(lengths, prev_offsets), -1)
    extra_keys = (
        jnp.concatenate([prev_keys, head_k[1]], axis=0),
        jnp.concatenate([prev_values, head_v[1]], axis=0),
        jnp.concatenate([prev_offsets, own_offsets], axis=0) + doc_len,
        jnp.concatenate([prev_seg, own_seg], axis=0),
    )
    half_rows = jnp.arange(half_len, dtype=jnp.int32)
    doc_seg = jnp.zeros((half_len,), jnp.int32)
    question_set = make_group(
        head_q[1],
        head_c[1],
        row_products(head_o[1], head_c[1], kv_local),
        own_offsets + doc_len,
        own_seg,
        kv_local,
    )
    lower_set = make_group(
        head_q[0][:half_len],
        head_c[0][:half_len],
        row_products(head_o[0][:half_len], head_c[0][:half_len], kv_local),
        ctx_pos * stretch_len + half_rows,
        doc_seg,
        kv_local,
    )
    upper_q = head_q[0][half_len:]
    upper_c = head_c[0][half_len:]
    upper_delta = row_products(head_o[0][half_len:], upper_c, kv_local)
    upper_pos = ctx_pos * stretch_len + half_len + half_rows
    upper_set = make_group(upper_q, upper_c, upper_delta, upper_pos, doc_seg, kv_local)
    question_set = with_log_sum(
        question_set, doc_keys, block_len, total_blocks, extra_keys, score_scale
    )
    lower_set = with_log_sum(lower_set, doc_keys, block_len, total_blocks, None, score_scale)
    upper_set = with_log_sum(upper_set, doc_keys, block_len, total_blocks, None, score_scale)
    doc_buffers = (
        jnp.zeros((doc_len, feat_width), jnp.float32),
        jnp.zeros((doc_len, feat_width), jnp.float32),
    )
    question_dq, doc_buffers, extra_grads = run_backward(
        question_set,
        doc_keys,
        doc_values,
        block_len,
        total_blocks,
        extra_keys,
        score_scale,
        doc_buffers,
    )
    lower_dq, doc_buffers, unused_lower = run_backward(
        lower_set, doc_keys, doc_values, block_len, total_blocks, None, score_scale, doc_buffers
    )
    upper_dq, doc_buffers, unused_upper = run_backward(
        upper_set, doc_keys, doc_values, block_len, total_blocks, None, score_scale, doc_buffers
    )
    doc_dk, doc_dv = (
        lax.psum_scatter(doc_buffers[0], "ctx", scatter_dimension=0, tiled=True),
        lax.psum_scatter(doc_buffers[1], "ctx", scatter_dimension=0, tiled=True),
    )
    back_key, back_value = (
        passed_along(extra_grads[0][:stretch_len].astype(jnp.bfloat16), "ctx", -1).astype(
            jnp.float32
        ),
        passed_along(extra_grads[1][:stretch_len].astype(jnp.bfloat16), "ctx", -1).astype(
            jnp.float32
        ),
    )
    question_dk = extra_grads[0][stretch_len:] + back_key
    question_dv = extra_grads[1][stretch_len:] + back_value
    query_width = head_q.shape[2]
    upper_low = upper_dq.reshape(half_len, query_width).astype(jnp.bfloat16)
    doc_dq = jnp.concatenate(
        [lower_dq.reshape(half_len, query_width).astype(jnp.bfloat16), upper_low], axis=0
    )
    question_low = question_dq.reshape(stretch_len, query_width).astype(jnp.bfloat16)
    grad_heads = jnp.stack([doc_dq, question_low], axis=0)
    grad_queries = lax.all_to_all(grad_heads, "head", split_axis=1, concat_axis=2, tiled=True)
    key_heads = jnp.stack([doc_dk, question_dk], axis=0)
    value_heads = jnp.stack([doc_dv, question_dv], axis=0)
    grad_keys, grad_values = (
        lax.all_to_all(key_heads, "head", split_axis=1, concat_axis=2, tiled=True),
        lax.all_to_all(value_heads, "head", split_axis=1, concat_axis=2, tiled=True),
    )
    return (grad_queries, grad_keys, grad_values)


def solution(mesh):
    in_specs = (
        P(None, ("ctx", "head"), None),
        P(None, ("ctx", "head"), None),
        P(None, ("ctx", "head"), None),
        P(None, ("ctx", "head"), None),
        P(None, ("ctx", "head"), None),
        P(),
    )
    out_specs = (
        P(None, ("ctx", "head"), None),
        P(None, ("ctx", "head"), None),
        P(None, ("ctx", "head"), None),
    )
    return jax.shard_map(shards, mesh=mesh, in_specs=in_specs, out_specs=out_specs, check_vma=False)
```

profile of v0, /device:TPU:4, one launch (start us, length us, event | category | flops | bytes accessed | tf_op | source)
XLA Modules:
  0.0 609.4 jit_solution(12818486736598552541)
XLA Ops:
  9.0 11.2 %all_to_all.129 = bf16[8,2,2048]{2,1,0:T(2,128)(2,1)S(1)} all-to-all(bf16[8,2,2048]{2,1,0:T(2,128)(2,1)S(1)} %reshape.760), channel_id=1, replica_groups=mesh['ctx'=32,'head'=8] {'head'}, dimensions={0} | all-to-all | bytes 131072 | tf_op jit(solution)/shard_map/all_to_all | solution.py:170
  23.2 3.4 all-to-all-start.2
  27.0 6.7 %copy.135 = bf16[2,16,8192]{1,0,2:T(2,128)(2,1)} copy(bf16[2,16,8192]{2,1,0:T(8,128)(2,1)S(1)} %copy-done.11) | data formatting | bytes 1048576 | tf_op args[3]
  33.7 6.5 %reshape.768 = bf16[8,2,16384]{2,1,0:T(2,128)(2,1)} reshape(bf16[8192,2,16]{2,1,0:T(2,128)(2,1)} %bitcast.634) | data formatting | bytes 1048576
  40.7 5.6 all-to-all-start.4
  56.1 6.7 %copy.127 = bf16[2,16,8192]{1,0,2:T(2,128)(2,1)} copy(bf16[2,16,8192]{2,1,0:T(8,128)(2,1)S(1)} %copy-done.12) | data formatting | bytes 1048576 | tf_op args[0]
  62.8 6.5 %reshape.762 = bf16[8,2,16384]{2,1,0:T(2,128)(2,1)} reshape(bf16[8192,2,16]{2,1,0:T(2,128)(2,1)} %bitcast.635) | data formatting | bytes 1048576
  69.3 6.7 %copy.133 = bf16[2,16,8192]{1,0,2:T(2,128)(2,1)} copy(bf16[2,16,8192]{2,1,0:T(8,128)(2,1)S(1)} %copy-done.13) | data formatting | bytes 1048576 | tf_op args[4]
  76.0 6.5 %reshape.766 = bf16[8,2,16384]{2,1,0:T(2,128)(2,1)} reshape(bf16[8192,2,16]{2,1,0:T(2,128)(2,1)} %bitcast.636) | data formatting | bytes 1048576
  82.7 1.9 collective-permute-start
  85.4 5.7 all-to-all-start.3
  91.8 4.1 reshape.769
  95.9 9.6 %copy.136 = bf16[2,16,8,1024]{3,0,1,2:T(2,128)(2,1)S(1)} copy(bf16[2,16,8,1024]{1,0,3,2:T(2,128)(2,1)} %bitcast.631) | data formatting | bytes 1048576 | tf_op jit(solution)/shard_map/all_to_all | solution.py:168
  105.9 5.7 all-to-all-start.1
  111.8 4.1 reshape.767
  116.0 8.9 %copy.134 = bf16[2,16,8,1024]{3,1,2,0:T(8,128)(2,1)S(1)} copy(bf16[2,16,8,1024]{1,0,3,2:T(2,128)(2,1)} %bitcast.632) | data formatting | bytes 1048576 | tf_op jit(solution)/shard_map/all_to_all | solution.py:169
  125.5 4.1 reshape.763
  129.6 8.9 %copy.128 = bf16[2,16,8,1024]{3,1,2,0:T(8,128)(2,1)S(1)} copy(bf16[2,16,8,1024]{1,0,3,2:T(2,128)(2,1)} %bitcast.633) | data formatting | bytes 1048576 | tf_op jit(solution)/shard_map/all_to_all | solution.py:167
  143.4 9.3 %while.86 = (s32[]{:T(128)}, f32[1,8,64]{2,1,0:T(8,128)S(1)}, f32[1,8,64]{2,1,0:T(8,128)S(1)}, s32[]{:T(128)}, bf16[4096,128]{1,0:T(8,128)(2,1)}, /*index=5*/bf1...) while((s32[]{:T(128)}, f32[1,8,64]{2,1,0:T(8,128)S(1)}, ...), condition=%wide.region_18.19_spmd.clone, body=%wide.region_15.18_spmd.clone.sunk | while | flops 68716104 | bytes 2488999 | solution.py:111
  143.5 1.4 select_reduce_fusion.10
  152.6 16.4 %while.84 = (s32[]{:T(128)}, f32[1,8,128]{2,1,0:T(8,128)S(1)}, f32[1,8,128]{2,1,0:T(8,128)S(1)}, s32[]{:T(128)}, bf16[4096,128]{1,0:T(8,128)(2,1)}, /*index=5*/b...) while((s32[]{:T(128)}, f32[1,8,128]{2,1,0:T(8,128)S(1)}, ...), condition=%wide.region_4.5_spmd.clone, body=%wide.region_1.0_spmd.clone.sunk | while | flops 137956096 | bytes 4842663 | solution.py:111
  154.9 1.4 fusion.213
  169.0 9.1 %while.88 = (s32[]{:T(128)}, f32[1,8,64]{2,1,0:T(8,128)S(1)}, f32[1,8,64]{2,1,0:T(8,128)S(1)}, s32[]{:T(128)}, bf16[4096,128]{1,0:T(8,128)(2,1)}, /*index=5*/bf1...) while((s32[]{:T(128)}, f32[1,8,64]{2,1,0:T(8,128)S(1)}, ...), condition=%wide.region_26.27_spmd.clone, body=%wide.region_23.26_spmd.clone.sunk | while | flops 68716104 | bytes 2488999 | solution.py:111
  179.2 1.4 broadcast.373
  180.6 54.6 %while.85 = (s32[]{:T(128)}, f32[128,1,8,128]{0,3,2,1:T(8,128)S(1)}, f32[4096,128]{1,0:T(8,128)}, f32[4096,128]{1,0:T(8,128)S(1)}, s32[]{:T(128)}, /*index=5*/bf...) while((s32[]{:T(128)}, ...), condition=%wide.region_13.14_spmd.clone, body=%wide.region_12.13_spmd.clone.sunk | while | flops 675283712 | bytes 13137147 | solution.py:151
  180.8 1.5 fusion.225
  185.3 2.1 fusion.228
  187.6 1.5 fusion.225
  192.2 2.1 fusion.228
  194.4 1.5 fusion.225
  199.0 2.1 fusion.228
  201.2 1.5 fusion.225
  205.8 2.1 fusion.228
  208.1 1.5 fusion.225
  212.6 2.1 fusion.228
  214.9 1.5 fusion.225
  219.5 2.1 fusion.228
  221.7 1.5 fusion.225
  226.3 2.1 fusion.228
  228.5 1.5 fusion.225
  233.1 2.1 fusion.228
  235.3 31.7 %while.87 = (s32[]{:T(128)}, f32[64,1,8,128]{3,0,2,1:T(8,128)S(1)}, f32[4096,128]{1,0:T(8,128)}, f32[4096,128]{1,0:T(8,128)S(1)}, s32[]{:T(128)}, /*index=5*/bf1...) while((s32[]{:T(128)}, f32[64,1,8,128]{3,0,2,1:T(8,128)S(1)}, ...), condition=%wide.region_21.22_spmd.clone, body=%wide.region_20.21_spmd.clone.sunk | while | flops 337740352 | bytes 7809787 | solution.py:151
  239.6 2.0 fusion.243
  246.0 2.0 fusion.243
  252.3 2.0 fusion.243
  258.6 2.0 fusion.243
  265.0 2.0 fusion.243
  267.0 31.1 %while.89 = (s32[]{:T(128)}, f32[64,1,8,128]{3,0,2,1:T(8,128)S(1)}, f32[4096,128]{1,0:T(8,128)}, f32[4096,128]{1,0:T(8,128)S(1)}, s32[]{:T(128)}, /*index=5*/bf1...) while((s32[]{:T(128)}, f32[64,1,8,128]{3,0,2,1:T(8,128)S(1)}, ...), condition=%wide.region_29.30_spmd.clone, body=%wide.region_28.29_spmd.clone.sunk | while | flops 337740352 | bytes 7283423 | solution.py:151
  271.3 2.0 fusion.258
  277.5 2.0 fusion.258
  283.7 2.0 fusion.258
  289.9 2.0 fusion.258
  296.1 2.0 fusion.258
  299.5 3.2 collective-permute-start.1
  302.7 1.6 convolution_bitcast_fusion.9
  304.3 6.3 %collective-permute-start.3 = (bf16[128,128]{1,0:T(8,128)(2,1)S(1)}, bf16[128,128]{1,0:T(8,128)(2,1)S(1)}, u32[]{:S(2)}, u32[]{:S(2)}) collective-permute-start(bf16[128,128]{1,0:T(8,128)(2,1)S(1)} %fusion.145), channel_id=1, source_target_pairs={{8,0},{16,8},{24,16},{32,24},{40,32},{48,40},{56,48},{64,56},{72,6... | collective-permute-start | bytes 98312 | tf_op jit(solution)/shard_map/ppermute | solution.py:17
  310.7 1.6 fusion.122
  312.6 1.9 collective-permute-start.2
  317.5 5.5 all-to-all-start.5
  323.0 144.1 %reduce-scatter.3.cloned.1.call-done = f32[128,128]{1,0:T(8,128)} async-done(((f32[4096,128]{1,0:T(8,128)}), f32[128,128]{1,0:T(8,128)}) %reduce-scatter.3.cloned.1.call-update) | async-done | bytes 65552 | tf_op jit(solution)/shard_map/reduce_scatter | solution.py:248
  468.7 4.9 all-to-all-start.6
  473.6 115.4 %reduce-scatter.5.cloned.1.call-done = f32[128,128]{1,0:T(8,128)} async-done(((f32[4096,128]{1,0:T(8,128)}), f32[128,128]{1,0:T(8,128)}) %reduce-scatter.5.cloned.1.call-update) | async-done | bytes 65552 | tf_op jit(solution)/shard_map/reduce_scatter | solution.py:249
  590.6 4.9 all-to-all-start.7
  597.2 4.9 all-to-all-done.7
  (435 shorter events, 124.7 us)
Async XLA Ops:
  7.2 14.4 %copy-start.17 = (bf16[2,16,1024]{2,1,0:T(8,128)(2,1)S(1)}, bf16[2,16,1024]{2,1,0:T(8,128)(2,1)}, u32[]{:S(2)}) copy-start(bf16[2,16,1024]{2,1,0:T(8,128)(2,1)} %param.20) | copy-start | bytes 196612
  7.2 19.4 %copy-start.19 = (s32[256]{0:T(256)S(1)}, s32[256]{0:T(256)}, u32[]{:S(2)}) copy-start(s32[256]{0:T(256)} %param.23) | copy-start | bytes 3076
  7.2 19.8 %copy-start.11 = (bf16[2,16,8192]{2,1,0:T(8,128)(2,1)S(1)}, bf16[2,16,8192]{2,1,0:T(8,128)(2,1)}, u32[]{:S(2)}) copy-start(bf16[2,16,8192]{2,1,0:T(8,128)(2,1)} %param.21) | copy-start | bytes 1572868
  7.2 136.1 %all-gather.3.cloned.1.call-start = ((), (), s32[]{:S(2)}) async-start(), calls=%async_computation.10 | async-start | bytes 1081344 | tf_op jit(solution)/shard_map/all_gather | solution.py:184
  23.2 17.5 %all-to-all-start.2 = ((bf16[8,2,2048]{2,1,0:T(2,128)(2,1)}), bf16[8,2,2048]{2,1,0:T(2,128)(2,1)S(1)}, u32[]{:S(2)}, u32[]{:S(2)}) async-start(bf16[8,2,2048]{2,1,0:T(2,128)(2,1)} %reshape.764), calls=%async_computation.2 | async-start | bytes 131072 | tf_op jit(solution)/shard_map/all_to_all | solution.py:171
  33.7 22.3 %copy-start.12 = (bf16[2,16,8192]{2,1,0:T(8,128)(2,1)S(1)}, bf16[2,16,8192]{2,1,0:T(8,128)(2,1)}, u32[]{:S(2)}) copy-start(bf16[2,16,8192]{2,1,0:T(8,128)(2,1)} %param.18) | copy-start | bytes 1572868
  40.7 44.7 %all-to-all-start.4 = ((bf16[8,2,16384]{2,1,0:T(2,128)(2,1)}), bf16[8,2,16384]{2,1,0:T(2,128)(2,1)S(1)}, u32[]{:S(2)}, u32[]{:S(2)}) async-start(bf16[8,2,16384]{2,1,0:T(2,128)(2,1)} %reshape.768), calls=%async_computation.4 | async-start | bytes 1048576 | tf_op jit(solution)/shard_map/all_to_all | solution.py:168
  62.8 6.5 %copy-start.13 = (bf16[2,16,8192]{2,1,0:T(8,128)(2,1)S(1)}, bf16[2,16,8192]{2,1,0:T(8,128)(2,1)}, u32[]{:S(2)}) copy-start(bf16[2,16,8192]{2,1,0:T(8,128)(2,1)} %param.22) | copy-start | bytes 1572868
  82.7 95.5 %copy-start.9 = (pred[128,256]{0,1:T(8,128)(4,1)}, pred[128,256]{0,1:T(8,128)(4,1)S(1)}, u32[]{:S(2)}) copy-start(pred[128,256]{0,1:T(8,128)(4,1)S(1)} %or_and_fusion) | copy-start | bytes 98308
  82.7 59.5 %collective-permute-start = (bf16[128,128]{1,0:T(8,128)(2,1)}, bf16[128,128]{1,0:T(8,128)(2,1)}, u32[]{:S(2)}, u32[]{:S(2)}) collective-permute-start(bf16[128,128]{1,0:T(8,128)(2,1)} %bitcast.7), channel_id=1, source_target_pairs={{0,8},{8,16},{16,24},{24,32},{32,40},{40,48},{48,56},{56,64},{64,7... | collective-permute-start | bytes 98312 | tf_op jit(solution)/shard_map/ppermute | solution.py:17
  85.4 20.5 %all-to-all-start.3 = ((bf16[8,2,16384]{2,1,0:T(2,128)(2,1)}), bf16[8,2,16384]{2,1,0:T(2,128)(2,1)S(1)}, u32[]{:S(2)}, u32[]{:S(2)}) async-start(bf16[8,2,16384]{2,1,0:T(2,128)(2,1)} %reshape.766), calls=%async_computation.3 | async-start | bytes 1048576 | tf_op jit(solution)/shard_map/all_to_all | solution.py:169
  91.1 87.9 %all-gather.5.cloned.1.call-start = ((), (), s32[]{:S(2)}) async-start(), calls=%async_computation.11 | async-start | bytes 1081344 | tf_op jit(solution)/shard_map/all_gather | solution.py:185
  105.9 19.6 %all-to-all-start.1 = ((bf16[8,2,16384]{2,1,0:T(2,128)(2,1)}), bf16[8,2,16384]{2,1,0:T(2,128)(2,1)S(1)}, u32[]{:S(2)}, u32[]{:S(2)}) async-start(bf16[8,2,16384]{2,1,0:T(2,128)(2,1)} %reshape.762), calls=%async_computation.1 | async-start | bytes 1048576 | tf_op jit(solution)/shard_map/all_to_all | solution.py:167
  111.6 355.5 %reduce-scatter.3.cloned.1.call-start = ((), (), s32[]{:S(2)}) async-start(), calls=%async_computation.12 | async-start | bytes 2162688 | tf_op jit(solution)/shard_map/reduce_scatter | solution.py:248
  138.7 1.4 copy-start.5
  139.0 2.5 copy-start.7
  140.1 3.2 copy-start.3
  143.3 34.9 %copy-start.2 = (f32[1,8,128,256]{2,3,1,0:T(8,128)}, f32[1,8,128,256]{2,3,1,0:T(8,128)S(1)}, u32[]{:S(2)}) copy-start(f32[1,8,128,256]{2,3,1,0:T(8,128)S(1)} %get-tuple-element.829) | copy-start | bytes 3145732
  180.6 1.6 copy-start.15
  187.5 1.6 copy-start.15
  194.3 1.6 copy-start.15
  201.1 1.6 copy-start.15
  207.9 1.6 copy-start.15
  214.7 1.6 copy-start.15
  221.6 1.6 copy-start.15
  228.4 1.6 copy-start.15
  235.2 31.7 %copy-start.14 = (f32[1,8,64]{2,1,0:T(8,128)S(1)}, f32[1,8,64]{2,1,0:T(8,128)}, u32[]{:S(2)}) copy-start(f32[1,8,64]{2,1,0:T(8,128)} %copy.151) | copy-start | bytes 6148
  235.4 3.9 copy-start.1
  241.7 3.9 copy-start.1
  248.1 3.9 copy-start.1
  254.4 3.9 copy-start.1
  260.7 3.9 copy-start.1
  298.1 1.3 copy-start
  298.1 1.4 copy-start.16
  298.1 4.6 copy-start.8
  298.1 4.6 copy-start.6
  298.1 4.6 copy-start.10
  298.1 4.6 copy-start.18
  298.2 290.8 %reduce-scatter.5.cloned.1.call-start = ((), (), s32[]{:S(2)}) async-start(), calls=%async_computation.13 | async-start | bytes 2162688 | tf_op jit(solution)/shard_map/reduce_scatter | solution.py:249
  299.5 12.8 %copy-start.4 = (bf16[16,8,8,128]{3,2,1,0:T(8,128)(2,1)S(1)}, bf16[16,8,8,128]{3,2,1,0:T(8,128)(2,1)}, u32[]{:S(2)}) copy-start(bf16[16,8,8,128]{3,2,1,0:T(8,128)(2,1)} %copy-done.3) | copy-start | bytes 786436
  299.5 11.2 %collective-permute-start.1 = (bf16[128,128]{1,0:T(8,128)(2,1)S(1)}, bf16[128,128]{1,0:T(8,128)(2,1)S(1)}, u32[]{:S(2)}, u32[]{:S(2)}) collective-permute-start(bf16[128,128]{1,0:T(8,128)(2,1)S(1)} %bitcast.688), channel_id=1, source_target_pairs={{0,8},{8,16},{16,24},{24,32},{32,40},{40,48},{48,56},{56,64},{64,7... | collective-permute-start | bytes 98312 | tf_op jit(solution)/shard_map/ppermute | solution.py:17
  304.3 18.6 %collective-permute-start.3 = (bf16[128,128]{1,0:T(8,128)(2,1)S(1)}, bf16[128,128]{1,0:T(8,128)(2,1)S(1)}, u32[]{:S(2)}, u32[]{:S(2)}) collective-permute-start(bf16[128,128]{1,0:T(8,128)(2,1)S(1)} %fusion.145), channel_id=1, source_target_pairs={{8,0},{16,8},{24,16},{32,24},{40,32},{48,40},{56,48},{64,56},{72,6... | collective-permute-start | bytes 98312 | tf_op jit(solution)/shard_map/ppermute | solution.py:17
  312.6 10.4 %collective-permute-start.2 = (bf16[128,128]{1,0:T(8,128)(2,1)S(1)}, bf16[128,128]{1,0:T(8,128)(2,1)S(1)}, u32[]{:S(2)}, u32[]{:S(2)}) collective-permute-start(bf16[128,128]{1,0:T(8,128)(2,1)S(1)} %fusion.144), channel_id=1, source_target_pairs={{8,0},{16,8},{24,16},{32,24},{40,32},{48,40},{56,48},{64,56},{72,6... | collective-permute-start | bytes 98312 | tf_op jit(solution)/shard_map/ppermute | solution.py:17
  317.5 151.2 %all-to-all-start.5 = ((bf16[2,128,1024]{2,0,1:T(2,128)(2,1)}), bf16[2,128,1024]{2,0,1:T(2,128)(2,1)S(1)}, u32[]{:S(2)}, u32[]{:S(2)}) async-start(bf16[2,128,1024]{2,0,1:T(2,128)(2,1)} %copy.158), calls=%async_computation.5 | async-start | bytes 1048576 | tf_op jit(solution)/shard_map/all_to_all | solution.py:268
  468.7 121.9 %all-to-all-start.6 = ((f32[2,128,128]{2,0,1:T(2,128)}), f32[2,128,128]{2,0,1:T(2,128)S(1)}, u32[]{:S(2)}, u32[]{:S(2)}) async-start(f32[2,128,128]{2,0,1:T(2,128)} %copy.162), calls=%async_computation.7 | async-start | bytes 262144 | tf_op jit(solution)/shard_map/all_to_all | solution.py:272
  590.6 11.5 %all-to-all-start.7 = ((f32[2,128,128]{2,0,1:T(2,128)}), f32[2,128,128]{2,0,1:T(2,128)S(1)}, u32[]{:S(2)}, u32[]{:S(2)}) async-start(f32[2,128,128]{2,0,1:T(2,128)} %copy.165), calls=%async_computation.9 | async-start | bytes 262144 | tf_op jit(solution)/shard_map/all_to_all | solution.py:273
Sparse Core Ops, SparseCore 0:
  21.7 76.6 all-gather.2
  101.2 74.3 all-gather.4
  298.3 168.7 reduce-scatter.2
  471.7 117.2 reduce-scatter.4
where the time goes:
time: 614 us; the launch traced here: 609 us
  waiting for transfers between devices  265 us (43%)
  matrix products  144 us (23%)
  local copies, waits for them, and re-layouts  97.4 us (16%)
  starting transfers between devices  49.4 us (8%)
  between operations  22.4 us (4%)
  other arithmetic  18.3 us (3%)
  blocking collectives  11.2 us (2%)
    reduce_scatter x1, waiting for transfers between devices, shards(): lax.psum_scatter(doc_buffers[0], 'ctx', scatter_dimension=0, tiled=True)  144 us
    reduce_scatter x1, waiting for transfers between devices, shards(): lax.psum_scatter(doc_buffers[1], 'ctx', scatter_dimension=0, tiled=True)  115 us
    unnamed x68, local copies, waits for them, and re-layouts  60.4 us
    dot_general x37, matrix products, block_scores(): jnp.einsum('rkgd,skd->kgrs', query_four, key_three, preferred_element_typ...  49.8 us
    dot_general x19, matrix products, block_backward(): jnp.einsum('kgrs,rkgd->skd', dscore, query_four, preferred_element_type=j...  37 us
    dot_general x19, matrix products, block_backward(): jnp.einsum('rkgd,skd->kgrs', cot_four, value_three, preferred_element_typ...  24.8 us
    dot_general x19, matrix products, block_backward(): jnp.einsum('kgrs,skd->rkgd', dscore, key_three, preferred_element_type=jn...  23.5 us
    ppermute x4, starting transfers between devices, passed_along(): lax.ppermute(value, axis, [(source, source + steps) for source in range(i...  13.4 us
  transfers between devices with their start and end apart: 15, of which 3 were waited for; matrix products, arithmetic and copies ran while one was open for 22% of the time, Pallas kernels for 0%

commit v1 on v0

v1 whole, which is shorter than its diff:
```python
import functools
import math

import jax
import jax.numpy as jnp
from jax import lax
from jax.experimental import pallas as pl
from jax.experimental.pallas import tpu as pltpu
from jax.sharding import PartitionSpec as P

HD = 128
NEG_FILL = -1e30
QMOST = 32
SCALE = HD ** (-0.5)
EXP2_SCALE = SCALE * math.log2(math.e)
MESH = pl.DeviceIdType.MESH
CHUNK = 256


def remote(src, dst, send_sem, recv_sem, device):
    return pltpu.make_async_remote_copy(
        src_ref=src,
        dst_ref=dst,
        send_sem=send_sem,
        recv_sem=recv_sem,
        device_id=device,
        device_id_type=MESH,
    )


class Place:
    def __init__(self, ctx_count, head_count):
        self.nctx = ctx_count
        self.nh = head_count
        self.nz = ctx_count // 4
        self.ctx = lax.axis_index("ctx")
        self.h = lax.axis_index("head")
        self.c = lax.rem(self.ctx, 2)
        self.z = lax.rem(self.ctx // 2, self.nz)
        self.xh = self.ctx // (2 * self.nz)
        half = self.nz // 2
        self.up = (half, half - 1)
        self.down = (half - 1, half)

    def zmod(self, z):
        return lax.rem(z + self.nz, self.nz)

    def block(self, xh, z, c):
        return (xh * self.nz + self.zmod(z)) * 2 + c

    def pair(self, xh, z):
        return xh * self.nz + self.zmod(z)

    def dev(self, xh, z, c):
        return (self.block(xh, z, c), self.h)

    def z_up(self):
        return self.dev(self.xh, self.z + 1, self.c)

    def z_down(self):
        return self.dev(self.xh, self.z - 1, self.c)

    def x_partner(self):
        return self.dev(1 - self.xh, self.z, self.c)

    def sibling(self):
        return self.dev(self.xh, self.z, 1 - self.c)

    def ctx_next(self):
        return (lax.rem(self.ctx + 1, self.nctx), self.h)

    def ctx_prev(self):
        return (lax.rem(self.ctx + self.nctx - 1, self.nctx), self.h)

    def head_peer(self, d):
        return lax.rem(self.h + d, self.nh)

    def head_source(self, d):
        return lax.rem(self.h + self.nh - d, self.nh)

    def barrier(self):
        barrier = pltpu.get_barrier_semaphore()

        def greet(d, _):
            pl.semaphore_signal(
                barrier, inc=1, device_id=(self.ctx, self.head_peer(d)), device_id_type=MESH
            )
            return 0

        lax.fori_loop(1, self.nh, greet, 0)
        near = (
            self.z_up(),
            self.z_down(),
            self.x_partner(),
            self.sibling(),
            self.ctx_next(),
            self.ctx_prev(),
        )
        for device in near:
            pl.semaphore_signal(barrier, inc=1, device_id=device, device_id_type=MESH)
        pl.semaphore_wait(barrier, self.nh - 1 + len(near))


def kernel_in(
    dims,
    q_ref,
    k_ref,
    v_ref,
    o_ref,
    c_ref,
    q_in,
    c_in,
    d_in,
    kvd,
    kvq,
    delta,
    kv_send,
    kv_recv,
    q_send,
    q_recv,
    c_send,
    c_recv,
    d_send,
    d_recv,
    g_send,
    g_recv,
    x_send,
    x_recv,
    local_sem,
):
    nctx, nh, tok, gw, bl, nhead = dims
    me = Place(nctx, nh)
    me.barrier()
    own_rows = pl.ds(pl.multiple_of(me.h * tok, tok), tok)

    def head_slice(ref, p, width):
        return ref.at[:, :, pl.ds(pl.multiple_of(p * width, width), width)]

    def kv_copies(d, p, device):
        copies = []
        for i, ref in enumerate((k_ref, v_ref)):
            cols = pl.ds(pl.multiple_of(p * HD, HD), HD)
            copies.append(
                remote(
                    ref.at[0, :, cols],
                    kvd.at[i, me.ctx, own_rows],
                    kv_send.at[2 * i, d],
                    kv_recv.at[2 * i, d],
                    device,
                )
            )
            copies.append(
                remote(
                    ref.at[1, :, cols],
                    kvq.at[i, 1, own_rows],
                    kv_send.at[2 * i + 1, d],
                    kv_recv.at[2 * i + 1, d],
                    device,
                )
            )
        return copies

    def q_copy(d, p, device):
        return remote(
            head_slice(q_ref, p, gw), q_in.at[:, me.h], q_send.at[d], q_recv.at[d], device
        )

    def c_copy(d, p, device):
        return remote(
            head_slice(c_ref, p, gw), c_in.at[:, me.h], c_send.at[d], c_recv.at[d], device
        )

    def d_copy(d, p, device):
        return remote(delta, d_in.at[:, me.h], d_send.at[d], d_recv.at[d], device)

    def over_peers(make, act):
        def step(d, _):
            p = me.head_peer(d)
            made = make(d, p, (me.ctx, p))
            for copy in made if isinstance(made, list) else [made]:
                act(copy)
            return 0

        lax.fori_loop(1, nh, step, 0)

    over_peers(kv_copies, lambda x: x.start())
    over_peers(q_copy, lambda x: x.start())
    over_peers(c_copy, lambda x: x.start())

    locals_ = []
    cols = pl.ds(pl.multiple_of(me.h * HD, HD), HD)
    for i, ref in enumerate((k_ref, v_ref)):
        locals_.append(
            pltpu.make_async_copy(
                ref.at[0, :, cols], kvd.at[i, me.ctx, own_rows], local_sem.at[2 * i]
            )
        )
        locals_.append(
            pltpu.make_async_copy(
                ref.at[1, :, cols], kvq.at[i, 1, own_rows], local_sem.at[2 * i + 1]
            )
        )
    locals_.append(
        pltpu.make_async_copy(head_slice(q_ref, me.h, gw), q_in.at[:, me.h], local_sem.at[4])
    )
    locals_.append(
        pltpu.make_async_copy(head_slice(c_ref, me.h, gw), c_in.at[:, me.h], local_sem.at[5])
    )
    for copy in locals_:
        copy.start()

    lanes = lax.broadcasted_iota(jnp.int32, (2, tok, HD), 2)

    def one_head(j, acc):
        at = pl.ds(pl.multiple_of(j * HD, HD), HD)
        prod = c_ref[:, :, at].astype(jnp.float32) * o_ref[:, :, at].astype(jnp.float32)
        return jnp.where(lanes == j, jnp.sum(prod, axis=-1, keepdims=True), acc)

    delta[...] = lax.fori_loop(0, nhead, one_head, jnp.zeros((2, tok, HD), jnp.float32))
    over_peers(d_copy, lambda x: x.start())
    own_delta = pltpu.make_async_copy(delta, d_in.at[:, me.h], local_sem.at[6])
    own_delta.start()

    for copy in locals_[:4]:
        copy.wait()

    def kv_arrived(d, _):
        for i in range(2):
            for j in range(2):
                dst = kvd.at[i, me.ctx, own_rows] if j == 0 else kvq.at[i, 1, own_rows]
                remote(
                    dst,
                    dst,
                    kv_send.at[2 * i + j, d],
                    kv_recv.at[2 * i + j, d],
                    (me.ctx, me.head_peer(d)),
                ).wait_recv()
        return 0

    lax.fori_loop(1, nh, kv_arrived, 0)

    tail = pl.ds(bl - QMOST, QMOST)
    tail_copy = remote(
        kvq.at[:, 1, tail], kvq.at[:, 0, tail], x_send, x_recv, me.ctx_next()
    )
    tail_copy.start()

    started = []

    def send(block, kind, device):
        copy = remote(
            kvd.at[:, block], kvd.at[:, block], g_send.at[kind, block], g_recv.at[block], device
        )
        copy.start()
        started.append(copy)

    def arrived(block):
        remote(
            kvd.at[:, block], kvd.at[:, block], g_send.at[0, block], g_recv.at[block], me.sibling()
        ).wait_recv()

    own = me.block(me.xh, me.z, me.c)
    other = me.block(1 - me.xh, me.z, me.c)
    send(own, 3, me.x_partner())
    send(own, 0, me.z_up())
    send(own, 1, me.z_down())
    send(own, 2, me.sibling())
    arrived(other)
    send(other, 0, me.z_up())
    send(other, 1, me.z_down())
    send(other, 2, me.sibling())
    for s in range(1, me.nz // 2 + 1):
        for xs in range(2):
            if s <= me.up[xs]:
                b = me.block(xs, me.z - s, me.c)
                arrived(b)
                if s < me.up[xs]:
                    send(b, 0, me.z_up())
                send(b, 2, me.sibling())
            if s <= me.down[xs]:
                b = me.block(xs, me.z + s, me.c)
                arrived(b)
                if s < me.down[xs]:
                    send(b, 1, me.z_down())
                send(b, 2, me.sibling())

    def from_sibling(i, _):
        arrived(2 * i + 1 - me.c)
        return 0

    lax.fori_loop(0, nctx // 2, from_sibling, 0)
    for copy in started:
        copy.wait_send()
    tail_copy.wait()
    for copy in locals_[4:]:
        copy.wait()
    own_delta.wait()
    over_peers(kv_copies, lambda x: x.wait_send())
    over_peers(q_copy, lambda x: x.wait())
    over_peers(c_copy, lambda x: x.wait())
    over_peers(d_copy, lambda x: x.wait())


def nt_dot(a, b):
    return lax.dot_general(a, b, (((1,), (1,)), ((), ())), preferred_element_type=jnp.float32)


def nn_dot(a, b):
    return jnp.dot(a, b, preferred_element_type=jnp.float32)


def kernel_mid(
    dims,
    len_ref,
    q_in,
    c_in,
    d_in,
    kvd,
    kvq,
    dq_out,
    dkv_out,
    dx_out,
    qs,
    cs,
    dd,
    weights,
    run_max,
    run_sum,
    tile_max,
    scale_inv,
    dqt,
    low_p,
    low_s,
    kx,
):
    nctx, nh, tok, gw, bl, nhead = dims
    ctx = lax.axis_index("ctx")
    h = lax.axis_index("head")
    group = gw // HD
    rows = group * bl
    npair = nctx // 2
    tile = 2 * bl
    own_pair = ctx // 2
    chunks = [pl.ds(r * CHUNK, CHUNK) for r in range(rows // CHUNK)]

    for s in range(2):
        for g in range(group):
            cols = slice(g * HD, (g + 1) * HD)
            qs[s, g * bl : (g + 1) * bl, :] = q_in[s, :, :, cols].reshape(bl, HD)
            cs[s, g * bl : (g + 1) * bl, :] = c_in[s, :, :, cols].reshape(bl, HD)
        turned = jnp.transpose(d_in[s].reshape(bl, HD))
        kx[0:HD, :] = turned
        mine = kx[pl.ds(pl.multiple_of(h * group, group), group), :]
        for g in range(group):
            dd[s, 0:1, g * bl : (g + 1) * bl] = mine[g : g + 1, :]

    count = len_ref.shape[1]
    lens = jnp.broadcast_to(len_ref[...].astype(jnp.float32), (8, count)).astype(jnp.bfloat16)
    i0 = lax.broadcasted_iota(jnp.int32, (count, count), 0)
    i1 = lax.broadcasted_iota(jnp.int32, (count, count), 1)
    before = jnp.where(i0 < i1, 1.0, 0.0).astype(jnp.bfloat16)
    after = jnp.where(i1 < i0, 1.0, 0.0).astype(jnp.bfloat16)
    starts_row = nn_dot(lens, before)[0:1, :]
    starts_col = nt_dot(after, lens)[:, 0:1]
    row_at = lax.broadcasted_iota(jnp.int32, (1, CHUNK), 1) % bl
    key_at = lax.broadcasted_iota(jnp.int32, (tile, 1), 0) - bl
    row_off = (row_at + ctx * bl).astype(jnp.float32)
    key_off = (key_at + ctx * bl).astype(jnp.float32)
    row_seg = jnp.sum(jnp.where(starts_col <= row_off, 1.0, 0.0), axis=0, keepdims=True)
    key_seg = jnp.sum(jnp.where(starts_row <= key_off, 1.0, 0.0), axis=1, keepdims=True)
    question_mask = (key_at <= row_at) & (key_seg == row_seg)
    doc_key = lax.broadcasted_iota(jnp.int32, (tile, 1), 0) + (own_pair * 2 - ctx) * bl
    doc_mask = doc_key <= row_at

    run_max[...] = jnp.full(run_max.shape, NEG_FILL, jnp.float32)
    run_sum[...] = jnp.zeros(run_sum.shape, jnp.float32)
    dqt[...] = jnp.zeros(dqt.shape, jnp.float32)

    def doc_kv(i, t):
        return kvd[i, pl.ds(2 * t, 2)].reshape(tile, HD)

    def question_kv(i):
        at = lax.broadcasted_iota(jnp.int32, (bl, HD), 0)
        prev = jnp.where(at >= bl - QMOST, kvq[i, 0].astype(jnp.float32), 0.0)
        return jnp.concatenate([prev.astype(jnp.bfloat16), kvq[i, 1]], axis=0)

    def first_pass(s, slot, keys, mask):
        for cols in chunks:
            scores = nt_dot(keys, qs[s, cols, :])
            if mask is not None:
                scores = jnp.where(mask, scores, NEG_FILL)
            old = run_max[s, 0:1, cols]
            new = jnp.maximum(old, jnp.max(scores, axis=0, keepdims=True))
            part = jnp.exp2((scores - new) * EXP2_SCALE)
            weights[slot, :, cols] = part
            run_sum[s, 0:1, cols] = run_sum[s, 0:1, cols] * jnp.exp2(
                (old - new) * EXP2_SCALE
            ) + jnp.sum(part, axis=0, keepdims=True)
            run_max[s, 0:1, cols] = new
            tile_max[slot, 0:1, cols] = new

    def slot_of(s, t):
        return s * (npair + 1) + t

    def pass_question(t, _):
        first_pass(1, npair + t, doc_kv(0, t), None)
        return 0

    def pass_doc(t, _):
        first_pass(0, t, doc_kv(0, t), None)
        return 0

    lax.fori_loop(0, npair, pass_question, 0)
    first_pass(1, 2 * npair, question_kv(0), question_mask)
    lax.fori_loop(0, own_pair, pass_doc, 0)
    first_pass(0, own_pair, doc_kv(0, own_pair), doc_mask)
    for s in range(2):
        scale_inv[s] = 1.0 / run_sum[s]

    def second_pass(s, slot, keys, values):
        for cols in chunks:
            factor = (
                jnp.exp2((tile_max[slot, 0:1, cols] - run_max[s, 0:1, cols]) * EXP2_SCALE)
                * scale_inv[s, 0:1, cols]
            )
            prob = weights[slot, :, cols] * factor
            d_prob = nt_dot(values, cs[s, cols, :])
            low_p[:, cols] = prob.astype(jnp.bfloat16)
            low_s[:, cols] = (prob * (d_prob - dd[s, 0:1, cols])).astype(jnp.bfloat16)
        d_value = nn_dot(low_p[...], cs[s])
        d_key = nn_dot(low_s[...], qs[s])
        keys_t = jnp.transpose(keys.astype(jnp.float32)).astype(jnp.bfloat16)
        dqt[s] += nn_dot(keys_t, low_s[...])
        return d_key, d_value

    def put(t, i, value, add):
        for c in range(2):
            part = value[c * bl : (c + 1) * bl]
            if add:
                part = dkv_out[t, i, c] + part
            dkv_out[t, i, c] = part

    def backward(t, _):
        keys, values = doc_kv(0, t), doc_kv(1, t)
        for i, value in enumerate(second_pass(1, npair + t, keys, values)):
            put(t, i, value, False)

        @pl.when(t <= own_pair)
        def _():
            for i, value in enumerate(second_pass(0, t, keys, values)):
                put(t, i, value, True)

        return 0

    lax.fori_loop(0, npair, backward, 0)
    d_key, d_value = second_pass(1, 2 * npair, question_kv(0), question_kv(1))
    dx_out[0] = d_key
    dx_out[1] = d_value
    for s in range(2):
        for g in range(group):
            part = jnp.transpose(dqt[s, :, g * bl : (g + 1) * bl])
            dq_out[s, :, g * HD : (g + 1) * HD] = (part * SCALE).astype(jnp.bfloat16)


def kernel_out(
    dims,
    dq,
    dkv,
    dx,
    gq,
    gk,
    gv,
    from_core,
    chain,
    from_x,
    from_next,
    sums,
    result,
    q_send,
    q_recv,
    core_send,
    core_recv,
    chain_send,
    chain_recv,
    x_send,
    x_recv,
    n_send,
    n_recv,
    r_send,
    r_recv,
    local_sem,
):
    nctx, nh, tok, gw, bl, nhead = dims
    npair = nctx // 2
    me = Place(nctx, nh)
    me.barrier()

    def rows_of(p):
        return pl.ds(pl.multiple_of(p * tok, tok), tok)

    q_cols = pl.ds(pl.multiple_of(me.h * gw, gw), gw)
    kv_cols = pl.ds(pl.multiple_of(me.h * HD, HD), HD)

    back = remote(
        dx.at[:, pl.ds(bl - QMOST, QMOST)], from_next, n_send, n_recv, me.ctx_prev()
    )
    back.start()
    core_copies = []

    def core_copy(t):
        return remote(
            dkv.at[t, :, 1 - me.c],
            from_core.at[t],
            core_send.at[t],
            core_recv.at[t],
            me.sibling(),
        )

    def core_start(t, _):
        core_copy(t).start()
        return 0

    lax.fori_loop(0, npair, core_start, 0)

    def q_copy(d):
        p = me.head_peer(d)
        return remote(
            dq.at[:, rows_of(p)], gq.at[:, :, q_cols], q_send.at[d], q_recv.at[d], (me.ctx, p)
        )

    def q_start(d, _):
        q_copy(d).start()
        return 0

    lax.fori_loop(1, nh, q_start, 0)
    own_q = pltpu.make_async_copy(dq.at[:, rows_of(me.h)], gq.at[:, :, q_cols], local_sem.at[0])
    own_q.start()

    def core_wait(t, _):
        core_copy(t).wait()
        sums[t] = dkv[t, :, me.c] + from_core[t]
        return 0

    lax.fori_loop(0, npair, core_wait, 0)

    started = []

    def hop(way, xs, j, src):
        copy = remote(
            src,
            chain.at[way, xs, j],
            chain_send.at[way, xs, j],
            chain_recv.at[way, xs, j],
            me.z_up() if way == 0 else me.z_down(),
        )
        copy.start()
        started.append(copy)

    def hop_arrived(way, xs, j):
        remote(
            chain.at[way, xs, j],
            chain.at[way, xs, j],
            chain_send.at[way, xs, j],
            chain_recv.at[way, xs, j],
            me.z_up(),
        ).wait_recv()

    length = (me.up, me.down)

    def target(way, xs, j):
        far = length[way][xs] - j
        return me.pair(xs, me.z + far if way == 0 else me.z - far)

    for way in range(2):
        for xs in range(2):
            hop(way, xs, 0, sums.at[target(way, xs, 0)])
    for j in range(1, me.nz // 2):
        for way in range(2):
            for xs in range(2):
                if j < length[way][xs]:
                    hop_arrived(way, xs, j - 1)
                    t = target(way, xs, j)
                    chain[way, xs, j - 1] += sums[t]
                    hop(way, xs, j, chain.at[way, xs, j - 1])
    for way in range(2):
        for xs in range(2):
            hop_arrived(way, xs, length[way][xs] - 1)
    for xs in range(2):
        t = me.pair(xs, me.z)
        sums[t] = (
            sums[t]
            + chain[0, xs, length[0][xs] - 1]
            + chain[1, xs, length[1][xs] - 1]
        )
    x_copy = remote(
        sums.at[me.pair(1 - me.xh, me.z)], from_x, x_send, x_recv, me.x_partner()
    )
    x_copy.start()
    back.wait()
    for i in range(2):
        factor = SCALE if i == 0 else 1.0
        result[i, 1, 0 : bl - QMOST] = dx[i, bl : 2 * bl - QMOST] * factor
        result[i, 1, bl - QMOST : bl] = (
            dx[i, 2 * bl - QMOST : 2 * bl] + from_next[i]
        ) * factor

    def r_copy(d, i, s):
        p = me.head_peer(d)
        return remote(
            result.at[i, s, rows_of(p)],
            (gk, gv)[i].at[s, :, kv_cols],
            r_send.at[2 * i + s, d],
            r_recv.at[2 * i + s, d],
            (me.ctx, p),
        )

    def own_r(i, s):
        return pltpu.make_async_copy(
            result.at[i, s, rows_of(me.h)],
            (gk, gv)[i].at[s, :, kv_cols],
            local_sem.at[1 + 2 * i + s],
        )

    def r_start(s):
        def step(d, _):
            for i in range(2):
                r_copy(d, i, s).start()
            return 0

        lax.fori_loop(1, nh, step, 0)
        for i in range(2):
            own_r(i, s).start()

    r_start(1)
    x_copy.wait()
    own = me.pair(me.xh, me.z)
    for i in range(2):
        factor = SCALE if i == 0 else 1.0
        result[i, 0] = (sums[own, i] + from_x[i]) * factor
    r_start(0)
    for copy in started:
        copy.wait_send()

    def ends(d, _):
        q_copy(d).wait()
        for i in range(2):
            for s in range(2):
                r_copy(d, i, s).wait()
        return 0

    lax.fori_loop(1, nh, ends, 0)
    own_q.wait()
    for i in range(2):
        for s in range(2):
            own_r(i, s).wait()


def shards(queries, keys, values, outputs, cotangent, lengths):
    nctx, nh = lax.axis_size("ctx"), lax.axis_size("head")
    tok = queries.shape[1]
    gw = queries.shape[2] // nh
    bl = tok * nh
    nhead = queries.shape[2] // HD
    dims = (nctx, nh, tok, gw, bl, nhead)
    npair = nctx // 2
    rows = gw // HD * bl
    hbm = pl.BlockSpec(memory_space=pl.ANY)
    vmem = pl.BlockSpec(memory_space=pltpu.VMEM)
    dma = pltpu.SemaphoreType.DMA
    f32, b16 = jnp.float32, jnp.bfloat16
    shape = jax.ShapeDtypeStruct
    q_in, c_in, d_in, kvd, kvq = pl.pallas_call(
        functools.partial(kernel_in, dims),
        out_shape=(
            shape((2, nh, tok, gw), b16),
            shape((2, nh, tok, gw), b16),
            shape((2, nh, tok, HD), f32),
            shape((2, nctx, bl, HD), b16),
            shape((2, 2, bl, HD), b16),
        ),
        in_specs=[hbm, hbm, hbm, vmem, vmem],
        out_specs=[hbm] * 5,
        scratch_shapes=[
            pltpu.VMEM((2, tok, HD), f32),
            dma((4, nh)),
            dma((4, nh)),
            dma((nh,)),
            dma((nh,)),
            dma((nh,)),
            dma((nh,)),
            dma((nh,)),
            dma((nh,)),
            dma((4, nctx)),
            dma((nctx,)),
            dma,
            dma,
            dma((7,)),
        ],
        compiler_params=pltpu.CompilerParams(collective_id=0, has_side_effects=True),
        name="exchange_in",
    )(queries, keys, values, outputs, cotangent)
    dq, dkv, dx = pl.pallas_call(
        functools.partial(kernel_mid, dims),
        out_shape=(
            shape((2, bl, gw), b16),
            shape((npair, 2, 2, bl, HD), f32),
            shape((2, 2 * bl, HD), f32),
        ),
        in_specs=[vmem] * 6,
        out_specs=[vmem] * 3,
        scratch_shapes=[
            pltpu.VMEM((2, rows, HD), b16),
            pltpu.VMEM((2, rows, HD), b16),
            pltpu.VMEM((2, 1, rows), f32),
            pltpu.VMEM((2 * npair + 1, 2 * bl, rows), f32),
            pltpu.VMEM((2, 1, rows), f32),
            pltpu.VMEM((2, 1, rows), f32),
            pltpu.VMEM((2 * npair + 1, 1, rows), f32),
            pltpu.VMEM((2, 1, rows), f32),
            pltpu.VMEM((2, HD, rows), f32),
            pltpu.VMEM((2 * bl, rows), b16),
            pltpu.VMEM((2 * bl, rows), b16),
            pltpu.VMEM((HD, bl), f32),
        ],
        compiler_params=pltpu.CompilerParams(vmem_limit_bytes=60 * 2**20),
        name="attention_backward",
    )(lengths.reshape(1, -1), q_in, c_in, d_in, kvd, kvq)
    steps = nctx // 8
    return pl.pallas_call(
        functools.partial(kernel_out, dims),
        out_shape=(
            shape((2, tok, nh * gw), b16),
            shape((2, tok, nh * HD), f32),
            shape((2, tok, nh * HD), f32),
        ),
        in_specs=[hbm, vmem, vmem],
        out_specs=[hbm] * 3,
        scratch_shapes=[
            pltpu.VMEM((npair, 2, bl, HD), f32),
            pltpu.VMEM((2, 2, steps, 2, bl, HD), f32),
            pltpu.VMEM((2, bl, HD), f32),
            pltpu.VMEM((2, QMOST, HD), f32),
            pltpu.VMEM((npair, 2, bl, HD), f32),
            pltpu.VMEM((2, 2, bl, HD), f32),
            dma((nh,)),
            dma((nh,)),
            dma((npair,)),
            dma((npair,)),
            dma((2, 2, steps)),
            dma((2, 2, steps)),
            dma,
            dma,
            dma,
            dma,
            dma((4, nh)),
            dma((4, nh)),
            dma((5,)),
        ],
        compiler_params=pltpu.CompilerParams(
            collective_id=1, has_side_effects=True, vmem_limit_bytes=40 * 2**20
        ),
        name="exchange_out",
    )(dq, dkv, dx)


def solution(mesh):
    spec = P(None, ("ctx", "head"), None)
    return jax.shard_map(
        shards,
        mesh=mesh,
        in_specs=(spec,) * 5 + (P(),),
        out_specs=(spec,) * 3,
        check_vma=False,
    )
```

time: 614 us -> 140 us (0.23)
  waiting for transfers between devices: 265 us -> 0 us
  matrix products: 144 us -> 0 us
  Pallas kernels: 0 us -> 133 us
  local copies, waits for them, and re-layouts: 97.4 us -> 6.28 us
  starting transfers between devices: 49.4 us -> 0 us
  between operations: 22.4 us -> 0.65 us
  other arithmetic: 18.3 us -> 0 us
  blocking collectives: 11.2 us -> 0 us
    reduce_scatter x2 -> x0, waiting for transfers between devices: 259 us -> none  [the longest x1 144 us: shards(): lax.psum_scatter(doc_buffers[0], 'ctx', scatter_dimension=0, tiled=True)]
    dot_general x113 -> x0, matrix products: 144 us -> none  [the longest x37 49.8 us: block_scores(): jnp.einsum('rkgd,skd->kgrs', query_four, key_three, preferred_element_typ...]
    pallas_call x0 -> x3, Pallas kernels: none -> 133 us  [the longest x1 51 us: shards(): pl.pallas_call(functools.partial(kernel_out, dims), out_shape=(shape((2,...]
    unnamed x68 -> x9, local copies, waits for them, and re-layouts: 60.4 us -> 6.28 us
    all_to_all x7 -> x0, starting transfers between devices: 35.7 us -> none  [the longest x1 5.71 us: shards(): lax.all_to_all(queries, 'head', split_axis=2, concat_axis=1, tiled=True)]
    all_to_all x11 -> x0, local copies, waits for them, and re-layouts: 30.5 us -> none  [the longest x1 9.59 us: shards(): lax.all_to_all(outputs, 'head', split_axis=2, concat_axis=1, tiled=True)]
    ppermute x4 -> x0, starting transfers between devices: 13.4 us -> none  [passed_along(): lax.ppermute(value, axis, [(source, source + steps) for source in range(i...]
    all_to_all x1 -> x0, blocking collectives: 11.2 us -> none  [shards(): lax.all_to_all(keys, 'head', split_axis=2, concat_axis=1, tiled=True)]
  transfers between devices with their start and end apart: 15 -> 0, of which waited for: 3 -> 0; matrix products, arithmetic and copies ran while one was open for 22% -> 0% of each run, Pallas kernels for 0% -> 0%
where the time goes in v1:
time: 140 us
  Pallas kernels  133 us (95%)
  local copies, waits for them, and re-layouts  6.28 us (4%)
    pallas_call x1, Pallas kernels, shards(): pl.pallas_call(functools.partial(kernel_out, dims), out_shape=(shape((2,...  51 us
    pallas_call x1, Pallas kernels, shards(): pl.pallas_call(functools.partial(kernel_in, dims), out_shape=(shape((2, n...  47.4 us
    pallas_call x1, Pallas kernels, shards(): pl.pallas_call(functools.partial(kernel_mid, dims), out_shape=(shape((2,...  34.8 us
    unnamed x9, local copies, waits for them, and re-layouts  6.28 us

profile of v1, /device:TPU:4, one launch (start us, length us, event | category | flops | bytes accessed | tf_op | source)
XLA Modules:
  0.0 140.1 jit_solution(11260856146939433848)
XLA Ops:
  0.6 47.4 %exchange_in.1 = (bf16[2,8,16,1024]{3,2,1,0:T(8,128)(2,1)}, bf16[2,8,16,1024]{3,2,1,0:T(8,128)(2,1)}, f32[2,8,16,128]{3,2,1,0:T(8,128)}, bf16[2,32,128,128]{3,2,1,0:T(8,128)(2,1)}, bf16[2,2,128,128]{3,2,1,0:T(8,128)(2,1)}) custom-call(bf16[2,16,8192]{2,1,0:T(8,128)(2,1)} %q_ref.1, bf16[2,16,1024]{2,1,0:T(8,128)(2,1)} %k_ref.1, bf16[2,16,1024]{2,1,0:T(8,128)(2,1)} %v_ref.1, ...), custom_call_target="tpu_custom_call" | custom-call | tf_op jit(solution)/shard_map/exchange_in/pallas_call | solution.py:672
  48.0 34.8 %attention_backward.1 = (bf16[2,128,1024]{2,1,0:T(8,128)(2,1)}, f32[16,2,2,128,128]{4,3,2,1,0:T(8,128)}, f32[2,256,128]{2,1,0:T(8,128)}) custom-call(s32[1,256]{1,0:T(1,128)} %bitcast.1, bf16[2,8,16,1024]{3,2,1,0:T(8,128)(2,1)} %get-tuple-element.11.q_in, bf16[2,8,16,1024]{3,2,1,0:T(8,128)(2,1)} %get-tuple-element.12.c_in, ...), custom_call_target="tpu_custom_call" | custom-call | tf_op jit(solution)/shard_map/attention_backward/pallas_call | solution.py:702
  82.8 0.0 copy-start
  82.8 2.2 %copy-done = f32[16,2,2,128,128]{4,3,2,1,0:T(8,128)S(1)} copy-done((f32[16,2,2,128,128]{4,3,2,1,0:T(8,128)S(1)}, f32[16,2,2,128,128]{4,3,2,1,0:T(8,128)}, u32[]{:S(2)}) %copy-start) | copy-done | bytes 4194328
  85.0 0.0 copy-start.1
  85.0 1.0 copy-done.1
  86.0 0.0 copy-start.2
  86.0 0.9 copy-done.2
  87.0 51.0 %exchange_out.1 = (bf16[2,16,8192]{2,1,0:T(8,128)(2,1)S(1)}, f32[2,16,1024]{2,1,0:T(8,128)S(1)}, f32[2,16,1024]{2,1,0:T(8,128)S(1)}) custom-call(bf16[2,128,1024]{2,1,0:T(8,128)(2,1)S(1)} %copy-done.1, f32[16,2,2,128,128]{4,3,2,1,0:T(8,128)S(1)} %copy-done, f32[2,256,128]{2,1,0:T(8,128)S(1)} %copy-done.2), custom_call_target="tpu_custom_call" | custom-call | tf_op jit(solution)/shard_map/exchange_out/pallas_call | solution.py:729
  138.0 0.8 copy.12
  138.8 0.7 copy.13
  139.5 0.7 copy.14
Async XLA Ops:
  82.8 2.2 %copy-start = (f32[16,2,2,128,128]{4,3,2,1,0:T(8,128)S(1)}, f32[16,2,2,128,128]{4,3,2,1,0:T(8,128)}, u32[]{:S(2)}) copy-start(f32[16,2,2,128,128]{4,3,2,1,0:T(8,128)} %get-tuple-element.17.dkv) | copy-start | bytes 12582916
  85.0 1.0 copy-start.1
  86.0 0.9 copy-start.2

commit v2 on v1

v2 whole, which is shorter than its diff:
```python
import functools
import math

import jax
import jax.numpy as jnp
from jax import lax
from jax.experimental import pallas as pl
from jax.experimental.pallas import tpu as pltpu
from jax.sharding import PartitionSpec as P

HD = 128
NEG_FILL = -1e30
QMOST = 32
SCALE = HD ** (-0.5)
EXP2_SCALE = SCALE * math.log2(math.e)
MESH = pl.DeviceIdType.MESH
CHUNK = 256
LAG = 2


def remote(src, dst, send_sem, recv_sem, device):
    return pltpu.make_async_remote_copy(
        src_ref=src,
        dst_ref=dst,
        send_sem=send_sem,
        recv_sem=recv_sem,
        device_id=device,
        device_id_type=MESH,
    )


class Place:
    def __init__(self, ctx_count, head_count):
        self.nctx = ctx_count
        self.nh = head_count
        self.nz = ctx_count // 4
        self.half = self.nz // 2
        self.npair = ctx_count // 2
        self.ctx = lax.axis_index("ctx")
        self.h = lax.axis_index("head")
        self.c = lax.rem(self.ctx, 2)
        self.z = lax.rem(self.ctx // 2, self.nz)
        self.xh = self.ctx // (2 * self.nz)

    def zmod(self, z):
        return lax.rem(z + self.nz, self.nz)

    def block(self, xh, z, c):
        return (xh * self.nz + self.zmod(z)) * 2 + c

    def pair(self, xh, z):
        return xh * self.nz + self.zmod(z)

    def dev(self, xh, z, c):
        return (self.block(xh, z, c), self.h)

    def z_up(self):
        return self.dev(self.xh, self.z + 1, self.c)

    def z_down(self):
        return self.dev(self.xh, self.z - 1, self.c)

    def x_partner(self):
        return self.dev(1 - self.xh, self.z, self.c)

    def sibling(self):
        return self.dev(self.xh, self.z, 1 - self.c)

    def ctx_next(self):
        return (lax.rem(self.ctx + 1, self.nctx), self.h)

    def ctx_prev(self):
        return (lax.rem(self.ctx + self.nctx - 1, self.nctx), self.h)

    def head_peer(self, d):
        return lax.rem(self.h + d, self.nh)

    def far(self, q):
        return self.half - q // 4

    def way(self, q):
        return q % 2

    def xs(self, q):
        return (q // 2 + q) % 2

    def reach(self, q):
        return self.half - (self.way(q) + self.xs(q) + 1) % 2

    def z_of(self, q):
        return self.z + self.far(q) * (1 - 2 * self.way(q))

    def pair_of(self, q):
        return self.pair(self.xs(q), self.z_of(q))

    def block_of(self, q, c):
        return self.block(self.xs(q), self.z_of(q), c)

    def barrier(self):
        barrier = pltpu.get_barrier_semaphore()

        def greet(d, _):
            pl.semaphore_signal(
                barrier, inc=1, device_id=(self.ctx, self.head_peer(d)), device_id_type=MESH
            )
            return 0

        lax.fori_loop(1, self.nh, greet, 0)
        near = (
            self.z_up(),
            self.z_down(),
            self.x_partner(),
            self.sibling(),
            self.ctx_next(),
            self.ctx_prev(),
        )
        for device in near:
            pl.semaphore_signal(barrier, inc=1, device_id=device, device_id_type=MESH)
        pl.semaphore_wait(barrier, self.nh - 1 + len(near))


def nt_dot(a, b):
    return lax.dot_general(a, b, (((1,), (1,)), ((), ())), preferred_element_type=jnp.float32)


def nn_dot(a, b):
    return jnp.dot(a, b, preferred_element_type=jnp.float32)


def by_sublane(x):
    return x.reshape(x.shape[0] // 8, 8, x.shape[1])


def kernel(
    dims,
    len_ref,
    q_ref,
    k_ref,
    v_ref,
    o_ref,
    c_ref,
    gq,
    gk,
    gv,
    q_in,
    c_in,
    d_in,
    kvd,
    kvq,
    delta,
    qs,
    cs,
    dd,
    turn,
    weights,
    peak,
    total,
    final_max,
    inverse,
    dqt,
    low_p,
    low_s,
    dkv,
    dx,
    dq,
    from_core,
    sums,
    chain,
    from_x,
    from_next,
    result,
    kv_send,
    kv_recv,
    q_send,
    q_recv,
    c_send,
    c_recv,
    d_send,
    d_recv,
    g_send,
    g_recv,
    t_send,
    t_recv,
    core_send,
    core_recv,
    hop_send,
    hop_recv,
    x_send,
    x_recv,
    n_send,
    n_recv,
    o_send,
    o_recv,
    r_send,
    r_recv,
    local_sem,
):
    nctx, nh, tok, gw, bl, nhead = dims
    me = Place(nctx, nh)
    npair = me.npair
    last = 4 * me.half + 1
    group = gw // HD
    rows = group * bl
    tile = 2 * bl
    own_pair = me.ctx // 2
    chunks = [pl.ds(r * CHUNK, CHUNK) for r in range(rows // CHUNK)]
    me.barrier()

    def rows_of(p):
        return pl.ds(pl.multiple_of(p * tok, tok), tok)

    own_rows = rows_of(me.h)

    def head_slice(ref, p, width):
        return ref.at[:, :, pl.ds(pl.multiple_of(p * width, width), width)]

    def over_peers(make, act):
        def step(d, _):
            p = me.head_peer(d)
            made = make(d, p, (me.ctx, p))
            for copy in made if isinstance(made, list) else [made]:
                act(copy)
            return 0

        lax.fori_loop(1, nh, step, 0)

    def start(copy):
        copy.start()

    def wait(copy):
        copy.wait()

    def wait_send(copy):
        copy.wait_send()

    def wait_recv(copy):
        copy.wait_recv()

    def kv_targets(i):
        return kvd.at[i, me.ctx, own_rows], kvq.at[i, 1, own_rows]

    def kv_copies(d, p, device):
        cols = pl.ds(pl.multiple_of(p * HD, HD), HD)
        return [
            remote(
                ref.at[j, :, cols],
                kv_targets(i)[j],
                kv_send.at[2 * i + j, d],
                kv_recv.at[2 * i + j, d],
                device,
            )
            for i, ref in enumerate((k_ref, v_ref))
            for j in range(2)
        ]

    def kv_arrivals(d, p, device):
        return [
            remote(
                kv_targets(i)[j],
                kv_targets(i)[j],
                kv_send.at[2 * i + j, d],
                kv_recv.at[2 * i + j, d],
                device,
            )
            for i in range(2)
            for j in range(2)
        ]

    def q_copy(d, p, device):
        return remote(
            head_slice(q_ref, p, gw), q_in.at[:, me.h], q_send.at[d], q_recv.at[d], device
        )

    def c_copy(d, p, device):
        return remote(
            head_slice(c_ref, p, gw), c_in.at[:, me.h], c_send.at[d], c_recv.at[d], device
        )

    def d_copy(d, p, device):
        return remote(delta, d_in.at[:, me.h], d_send.at[d], d_recv.at[d], device)

    over_peers(kv_copies, start)
    over_peers(q_copy, start)
    over_peers(c_copy, start)

    own_cols = pl.ds(pl.multiple_of(me.h * HD, HD), HD)
    locals_ = [
        pltpu.make_async_copy(ref.at[j, :, own_cols], kv_targets(i)[j], local_sem.at[2 * i + j])
        for i, ref in enumerate((k_ref, v_ref))
        for j in range(2)
    ]
    own_q = pltpu.make_async_copy(head_slice(q_ref, me.h, gw), q_in.at[:, me.h], local_sem.at[4])
    own_c = pltpu.make_async_copy(head_slice(c_ref, me.h, gw), c_in.at[:, me.h], local_sem.at[5])
    for copy in locals_:
        copy.start()
    own_q.start()
    own_c.start()
    for copy in locals_:
        copy.wait()
    over_peers(kv_arrivals, wait_recv)

    def gather_copy(b, kind, device):
        return remote(
            kvd.at[:, b], kvd.at[:, b], g_send.at[kind, b], g_recv.at[b], device
        )

    sent = []

    def send_block(b, kind, device):
        copy = gather_copy(b, kind, device)
        copy.start()
        sent.append(copy)

    def arrived(b):
        gather_copy(b, 0, me.sibling()).wait_recv()

    tail = pl.ds(bl - QMOST, QMOST)
    tail_copy = remote(kvq.at[:, 1, tail], kvq.at[:, 0, tail], t_send, t_recv, me.ctx_next())

    def gather_own(b):
        send_block(b, 0, me.z_up())
        send_block(b, 1, me.z_down())
        send_block(b, 2, me.sibling())

    def gather_step(q):
        b = me.block_of(q, me.c)
        arrived(b)
        if me.far(q) < me.reach(q):
            send_block(b, me.way(q), me.z_down() if me.way(q) == 0 else me.z_up())
        send_block(b, 2, me.sibling())

    send_block(me.ctx, 3, me.x_partner())
    gather_own(me.ctx)
    tail_copy.start()

    lanes = lax.broadcasted_iota(jnp.int32, (2, tok, HD), 2)

    def one_head(j, acc):
        at = pl.ds(pl.multiple_of(j * HD, HD), HD)
        prod = c_ref[:, :, at].astype(jnp.float32) * o_ref[:, :, at].astype(jnp.float32)
        return jnp.where(lanes == j, jnp.sum(prod, axis=-1, keepdims=True), acc)

    delta[...] = lax.fori_loop(0, nhead, one_head, jnp.zeros((2, tok, HD), jnp.float32))
    over_peers(d_copy, start)
    own_delta = pltpu.make_async_copy(delta, d_in.at[:, me.h], local_sem.at[6])
    own_delta.start()

    other = me.block(1 - me.xh, me.z, me.c)
    arrived(other)
    gather_own(other)

    count = len_ref.shape[1]
    lens = jnp.broadcast_to(len_ref[...].astype(jnp.float32), (8, count)).astype(jnp.bfloat16)
    i0 = lax.broadcasted_iota(jnp.int32, (count, count), 0)
    i1 = lax.broadcasted_iota(jnp.int32, (count, count), 1)
    before = jnp.where(i0 < i1, 1.0, 0.0).astype(jnp.bfloat16)
    after = jnp.where(i1 < i0, 1.0, 0.0).astype(jnp.bfloat16)
    starts_row = nn_dot(lens, before)[0:1, :]
    starts_col = nt_dot(after, lens)[:, 0:1]
    row_at = lax.broadcasted_iota(jnp.int32, (1, CHUNK), 1) % bl
    key_at = lax.broadcasted_iota(jnp.int32, (tile, 1), 0) - bl
    row_off = (row_at + me.ctx * bl).astype(jnp.float32)
    key_off = (key_at + me.ctx * bl).astype(jnp.float32)
    row_seg = jnp.sum(jnp.where(starts_col <= row_off, 1.0, 0.0), axis=0, keepdims=True)
    key_seg = jnp.sum(jnp.where(starts_row <= key_off, 1.0, 0.0), axis=1, keepdims=True)
    question_mask = (key_at <= row_at) & (key_seg == row_seg)
    doc_key = lax.broadcasted_iota(jnp.int32, (tile, 1), 0) + (own_pair * 2 - me.ctx) * bl
    doc_mask = doc_key <= row_at

    peak[...] = jnp.full(peak.shape, NEG_FILL, jnp.float32)
    total[...] = jnp.zeros(total.shape, jnp.float32)
    dqt[...] = jnp.zeros(dqt.shape, jnp.float32)

    def doc_kv(i, t):
        return kvd[i, pl.ds(2 * t, 2)].reshape(tile, HD)

    def question_kv(i):
        at = lax.broadcasted_iota(jnp.int32, (bl, HD), 0)
        prev = jnp.where(at >= bl - QMOST, kvq[i, 0].astype(jnp.float32), 0.0)
        return jnp.concatenate([prev.astype(jnp.bfloat16), kvq[i, 1]], axis=0)

    def scores_of(s, keys, mask, cols):
        scores = nt_dot(keys, qs[s, cols, :])
        return scores if mask is None else jnp.where(mask, scores, NEG_FILL)

    def peak_sweep(s, keys, mask):
        for cols in chunks:
            scores = by_sublane(scores_of(s, keys, mask, cols))
            peak[s, :, cols] = jnp.maximum(peak[s, :, cols], jnp.max(scores, axis=0))

    def weight_sweep(s, slot, keys, mask):
        for cols in chunks:
            scores = scores_of(s, keys, mask, cols)
            part = jnp.exp2((scores - final_max[s, 0:1, cols]) * EXP2_SCALE)
            weights[slot, :, cols] = part
            total[s, :, cols] = total[s, :, cols] + jnp.sum(by_sublane(part), axis=0)

    def on_pair(t, question, doc):
        question(None)

        @pl.when(t < own_pair)
        def _():
            doc(None)

        @pl.when(t == own_pair)
        def _():
            doc(doc_mask)

    for q in range(4 * me.half - 1, 4 * me.half - 5, -1):
        gather_step(q)
    for q in range(4 * me.half - 5, max(4 * me.half - 9, 1), -1):
        gather_step(q)

    own_q.wait()
    over_peers(q_copy, wait_recv)
    for s in range(2):
        for g in range(group):
            cols = slice(g * HD, (g + 1) * HD)
            qs[s, g * bl : (g + 1) * bl, :] = q_in[s, :, :, cols].reshape(bl, HD)

    def peaks(first, count):
        def step(i, _):
            q = first - i
            arrived(me.block_of(q, 1 - me.c))
            t = me.pair_of(q)
            keys = doc_kv(0, t)
            on_pair(
                t, lambda m: peak_sweep(1, keys, m), lambda m: peak_sweep(0, keys, m)
            )
            return 0

        lax.fori_loop(0, count, step, 0)

    peaks(last, 2)
    tail_copy.wait_recv()
    peak_sweep(1, question_kv(0), question_mask)
    peaks(last - 2, 4)
    for f in range(3, me.half + 1):
        top = last - 2 - 4 * (f - 1)
        for q in range(top, max(top - 4, 1), -1):
            gather_step(q)
        peaks(top + 4, 4)
    peaks(3 if me.half > 1 else 1, 2)

    for s in range(2):
        final_max[s] = jnp.max(peak[s], axis=0, keepdims=True)

    def weigh(t, _):
        keys = doc_kv(0, t)
        on_pair(
            t,
            lambda m: weight_sweep(1, npair + t, keys, m),
            lambda m: weight_sweep(0, t, keys, m),
        )
        return 0

    lax.fori_loop(0, npair, weigh, 0)
    weight_sweep(1, 2 * npair, question_kv(0), question_mask)
    for s in range(2):
        inverse[s] = 1.0 / jnp.sum(total[s], axis=0, keepdims=True)

    own_c.wait()
    own_delta.wait()
    over_peers(c_copy, wait_recv)
    over_peers(d_copy, wait_recv)
    for s in range(2):
        for g in range(group):
            cols = slice(g * HD, (g + 1) * HD)
            cs[s, g * bl : (g + 1) * bl, :] = c_in[s, :, :, cols].reshape(bl, HD)
        turn[...] = jnp.transpose(d_in[s].reshape(bl, HD))
        mine = turn[pl.ds(pl.multiple_of(me.h * group, group), group), :]
        for g in range(group):
            dd[s, 0:1, g * bl : (g + 1) * bl] = mine[g : g + 1, :]

    def backward(s, slot, keys, values):
        for cols in chunks:
            prob = weights[slot, :, cols] * inverse[s, 0:1, cols]
            d_prob = nt_dot(values, cs[s, cols, :])
            low_p[:, cols] = prob.astype(jnp.bfloat16)
            low_s[:, cols] = (prob * (d_prob - dd[s, 0:1, cols])).astype(jnp.bfloat16)
        d_value = nn_dot(low_p[...], cs[s])
        d_key = nn_dot(low_s[...], qs[s])
        keys_t = jnp.transpose(keys.astype(jnp.float32)).astype(jnp.bfloat16)
        dqt[s] += nn_dot(keys_t, low_s[...])
        return d_key, d_value

    def put(t, i, value, add):
        for c in range(2):
            part = value[c * bl : (c + 1) * bl]
            dkv[t, i, c] = dkv[t, i, c] + part if add else part

    def core_copy(t):
        return remote(
            dkv.at[t, :, 1 - me.c],
            from_core.at[t],
            core_send.at[t],
            core_recv.at[t],
            me.sibling(),
        )

    def hop_copy(way, xs, f):
        return remote(
            sums.at[me.pair(xs, me.z + f * (1 - 2 * way))],
            chain.at[way, xs, f - 1],
            hop_send.at[way, xs, f - 1],
            hop_recv.at[way, xs, f - 1],
            me.dev(me.xh, me.z + 1 - 2 * way, me.c),
        )

    def serve(q):
        f, way, xs, t = me.far(q), me.way(q), me.xs(q), me.pair_of(q)
        core_copy(t).wait_recv()
        sums[t] = dkv[t, :, me.c] + from_core[t]

        @pl.when((f > 0) & (f < me.reach(q)))
        def _():
            hop_copy(way, xs, f + 1).wait_recv()
            sums[t] = sums[t] + chain[way, xs, f]

        @pl.when(f > 0)
        def _():
            hop_copy(way, xs, f).start()

    def backward_pair(n, _):
        q = n + 2
        t = me.pair_of(q)
        keys, values = doc_kv(0, t), doc_kv(1, t)
        for i, value in enumerate(backward(1, npair + t, keys, values)):
            put(t, i, value, False)

        @pl.when(t <= own_pair)
        def _():
            for i, value in enumerate(backward(0, t, keys, values)):
                put(t, i, value, True)

        core_copy(t).start()

        @pl.when(n >= LAG)
        def _():
            serve(q - LAG)

        return 0

    lax.fori_loop(0, npair, backward_pair, 0)
    d_key, d_value = backward(1, 2 * npair, question_kv(0), question_kv(1))
    dx[0] = d_key
    dx[1] = d_value
    next_copy = remote(dx.at[:, tail], from_next, n_send, n_recv, me.ctx_prev())
    next_copy.start()

    for s in range(2):
        for g in range(group):
            part = jnp.transpose(dqt[s, :, g * bl : (g + 1) * bl])
            dq[s, :, g * HD : (g + 1) * HD] = (part * SCALE).astype(jnp.bfloat16)

    q_cols = pl.ds(pl.multiple_of(me.h * gw, gw), gw)

    def out_copy(d, p, device):
        return remote(
            dq.at[:, rows_of(p)], gq.at[:, :, q_cols], o_send.at[d], o_recv.at[d], device
        )

    own_out = pltpu.make_async_copy(dq.at[:, own_rows], gq.at[:, :, q_cols], local_sem.at[4])

    def serve_rest(n, _):
        serve(n + 2)
        return 0

    lax.fori_loop(npair - LAG, npair, serve_rest, 0)

    for way in range(2):
        for xs in range(2):
            hop_copy(way, xs, 1).wait_recv()
    for xs in range(2):
        t = me.pair(xs, me.z)
        sums[t] = sums[t] + chain[0, xs, 0] + chain[1, xs, 0]
    x_copy = remote(
        sums.at[me.pair(1 - me.xh, me.z)], from_x, x_send, x_recv, me.x_partner()
    )
    x_copy.start()
    over_peers(out_copy, start)
    own_out.start()
    next_copy.wait_recv()
    for i in range(2):
        factor = SCALE if i == 0 else 1.0
        result[i, 1, 0 : bl - QMOST] = dx[i, bl : 2 * bl - QMOST] * factor
        result[i, 1, bl - QMOST : bl] = (
            dx[i, 2 * bl - QMOST : 2 * bl] + from_next[i]
        ) * factor

    def r_copies(s):
        def made(d, p, device):
            return [
                remote(
                    result.at[i, s, rows_of(p)],
                    (gk, gv)[i].at[s, :, own_cols],
                    r_send.at[2 * i + s, d],
                    r_recv.at[2 * i + s, d],
                    device,
                )
                for i in range(2)
            ]

        return made

    def own_r(i, s):
        return pltpu.make_async_copy(
            result.at[i, s, own_rows], (gk, gv)[i].at[s, :, own_cols], local_sem.at[2 * i + s]
        )

    over_peers(r_copies(1), start)
    for i in range(2):
        own_r(i, 1).start()
    x_copy.wait_recv()
    own = me.pair(me.xh, me.z)
    for i in range(2):
        factor = SCALE if i == 0 else 1.0
        result[i, 0] = (sums[own, i] + from_x[i]) * factor
    over_peers(r_copies(0), start)
    for i in range(2):
        own_r(i, 0).start()

    for copy in sent:
        copy.wait_send()
    for make in (kv_copies, q_copy, c_copy, d_copy):
        over_peers(make, wait_send)
    tail_copy.wait_send()

    def core_done(t, _):
        core_copy(t).wait_send()
        return 0

    lax.fori_loop(0, npair, core_done, 0)
    for way in range(2):
        for xs in range(2):
            for f in range(1, me.half + (way + xs) % 2):
                hop_copy(way, xs, f).wait_send()
    x_copy.wait_send()
    next_copy.wait_send()
    for make in (out_copy, r_copies(0), r_copies(1)):
        over_peers(make, wait)
    own_out.wait()
    for i in range(2):
        for s in range(2):
            own_r(i, s).wait()


def shards(queries, keys, values, outputs, cotangent, lengths):
    nctx, nh = lax.axis_size("ctx"), lax.axis_size("head")
    tok = queries.shape[1]
    gw = queries.shape[2] // nh
    bl = tok * nh
    nhead = queries.shape[2] // HD
    dims = (nctx, nh, tok, gw, bl, nhead)
    npair = nctx // 2
    rows = gw // HD * bl
    hbm = pl.BlockSpec(memory_space=pl.ANY)
    vmem = pl.BlockSpec(memory_space=pltpu.VMEM)
    dma = pltpu.SemaphoreType.DMA
    space = pltpu.VMEM
    f32, b16 = jnp.float32, jnp.bfloat16
    shape = jax.ShapeDtypeStruct
    hops = nctx // 8
    return pl.pallas_call(
        functools.partial(kernel, dims),
        out_shape=(
            shape((2, tok, nh * gw), b16),
            shape((2, tok, nh * HD), f32),
            shape((2, tok, nh * HD), f32),
        ),
        in_specs=[vmem, hbm, hbm, hbm, vmem, vmem],
        out_specs=[hbm] * 3,
        scratch_shapes=[
            space((2, nh, tok, gw), b16),
            space((2, nh, tok, gw), b16),
            space((2, nh, tok, HD), f32),
            space((2, nctx, bl, HD), b16),
            space((2, 2, bl, HD), b16),
            space((2, tok, HD), f32),
            space((2, rows, HD), b16),
            space((2, rows, HD), b16),
            space((2, 1, rows), f32),
            space((HD, bl), f32),
            space((2 * npair + 1, 2 * bl, rows), f32),
            space((2, 8, rows), f32),
            space((2, 8, rows), f32),
            space((2, 1, rows), f32),
            space((2, 1, rows), f32),
            space((2, HD, rows), f32),
            space((2 * bl, rows), b16),
            space((2 * bl, rows), b16),
            space((npair, 2, 2, bl, HD), f32),
            space((2, 2 * bl, HD), f32),
            space((2, bl, gw), b16),
            space((npair, 2, bl, HD), f32),
            space((npair, 2, bl, HD), f32),
            space((2, 2, hops, 2, bl, HD), f32),
            space((2, bl, HD), f32),
            space((2, QMOST, HD), f32),
            space((2, 2, bl, HD), f32),
            dma((4, nh)),
            dma((4, nh)),
            dma((nh,)),
            dma((nh,)),
            dma((nh,)),
            dma((nh,)),
            dma((nh,)),
            dma((nh,)),
            dma((4, nctx)),
            dma((nctx,)),
            dma,
            dma,
            dma((npair,)),
            dma((npair,)),
            dma((2, 2, hops)),
            dma((2, 2, hops)),
            dma,
            dma,
            dma,
            dma,
            dma((nh,)),
            dma((nh,)),
            dma((4, nh)),
            dma((4, nh)),
            dma((7,)),
        ],
        compiler_params=pltpu.CompilerParams(
            collective_id=0, has_side_effects=True, vmem_limit_bytes=60 * 2**20
        ),
        name="attention_backward",
    )(lengths.reshape(1, -1), queries, keys, values, outputs, cotangent)


def solution(mesh):
    spec = P(None, ("ctx", "head"), None)
    return jax.shard_map(
        shards,
        mesh=mesh,
        in_specs=(spec,) * 5 + (P(),),
        out_specs=(spec,) * 3,
        check_vma=False,
    )
```

time: 140 us -> 105 us (0.75)
  Pallas kernels: 133 us -> 101 us
  local copies, waits for them, and re-layouts: 6.28 us -> 3.51 us
    pallas_call x3 -> x1, Pallas kernels: 133 us -> 101 us  [shards(): pl.pallas_call(functools.partial(kernel, dims), out_shape=(shape((2, tok,...]
    unnamed x9 -> x7, local copies, waits for them, and re-layouts: 6.28 us -> 3.51 us
where the time goes in v2:
time: 105 us
  Pallas kernels  101 us (96%)
  local copies, waits for them, and re-layouts  3.51 us (3%)
    pallas_call x1, Pallas kernels, shards(): pl.pallas_call(functools.partial(kernel, dims), out_shape=(shape((2, tok,...  101 us
    unnamed x7, local copies, waits for them, and re-layouts  3.51 us

profile of v2, /device:TPU:4, one launch (start us, length us, event | category | flops | bytes accessed | tf_op | source)
XLA Modules:
  0.0 104.9 jit_solution(14521188308561531559)
XLA Ops:
  0.6 100.8 %attention_backward.1 = (bf16[2,16,8192]{2,1,0:T(8,128)(2,1)}, f32[2,16,1024]{2,1,0:T(8,128)}, f32[2,16,1024]{2,1,0:T(8,128)}) custom-call(s32[1,256]{1,0:T(1,128)} %bitcast.1, bf16[2,16,8192]{2,1,0:T(8,128)(2,1)} %q_ref.1, bf16[2,16,1024]{2,1,0:T(8,128)(2,1)} %k_ref.1, bf16[2,16,1024]{2,1,0:T(8,128)(2,1)} %v_ref.1, bf16[2,16,8192]{2,1,0:T(8,128)(2,1)} %o_ref.1, ...), custom_call_target="tpu_custom_call" | custom-call | tf_op jit(solution)/shard_map/attention_backward/pallas_call | solution.py:664
  101.4 0.0 copy-start.1
  101.4 1.9 %copy.12 = bf16[2,16,8192]{2,1,0:T(8,128)(2,1)} copy(bf16[2,16,8192]{2,1,0:T(8,128)(2,1)} %get-tuple-element.6) | data formatting | bytes 1048576
  103.3 0.0 copy-done.1
  103.3 0.0 copy-start
  103.3 0.7 copy.13
  104.0 0.3 copy-done
  104.3 0.7 copy.14
Async XLA Ops:
  101.4 1.9 %copy-start.1 = (f32[2,16,1024]{2,1,0:T(8,128)S(1)}, f32[2,16,1024]{2,1,0:T(8,128)}, u32[]{:S(2)}) copy-start(f32[2,16,1024]{2,1,0:T(8,128)} %get-tuple-element.7) | copy-start | bytes 393220
  103.3 1.0 copy-start

commit v3 on v2

--- a/solution.py
+++ b/solution.py
@@ -16,6 +16,8 @@
 MESH = pl.DeviceIdType.MESH
 CHUNK = 256
 LAG = 2
+UNROLL = 4
+WIDE = 2
 
 
 def remote(src, dst, send_sem, recv_sem, device):
@@ -60,8 +62,8 @@
     def z_down(self):
         return self.dev(self.xh, self.z - 1, self.c)
 
-    def x_partner(self):
-        return self.dev(1 - self.xh, self.z, self.c)
+    def across(self):
+        return self.block(1 - self.xh, self.z, self.c)
 
     def sibling(self):
         return self.dev(self.xh, self.z, 1 - self.c)
@@ -105,18 +107,23 @@
             )
             return 0
 
+        def greet_across(d, _):
+            device = (self.across(), self.head_peer(d))
+            pl.semaphore_signal(barrier, inc=1, device_id=device, device_id_type=MESH)
+            return 0
+
         lax.fori_loop(1, self.nh, greet, 0)
+        lax.fori_loop(0, self.nh, greet_across, 0)
         near = (
             self.z_up(),
             self.z_down(),
-            self.x_partner(),
             self.sibling(),
             self.ctx_next(),
             self.ctx_prev(),
         )
         for device in near:
             pl.semaphore_signal(barrier, inc=1, device_id=device, device_id_type=MESH)
-        pl.semaphore_wait(barrier, self.nh - 1 + len(near))
+        pl.semaphore_wait(barrier, 2 * self.nh - 1 + len(near))
 
 
 def nt_dot(a, b):
@@ -165,12 +172,20 @@
     dq,
     from_core,
     sums,
+    low_sums,
     chain,
-    from_x,
+    low_chain,
     from_next,
     result,
+    final,
+    landed,
+    owned,
+    o_in,
+    c_near,
     kv_send,
     kv_recv,
+    kx_send,
+    kx_recv,
     q_send,
     q_recv,
     c_send,
@@ -185,14 +200,14 @@
     core_recv,
     hop_send,
     hop_recv,
-    x_send,
-    x_recv,
     n_send,
     n_recv,
     o_send,
     o_recv,
     r_send,
     r_recv,
+    f_send,
+    f_recv,
     local_sem,
 ):
     nctx, nh, tok, gw, bl, nhead = dims
@@ -204,6 +219,10 @@
     tile = 2 * bl
     own_pair = me.ctx // 2
     chunks = [pl.ds(r * CHUNK, CHUNK) for r in range(rows // CHUNK)]
+    fetch_o = pltpu.make_async_copy(o_ref, o_in, local_sem.at[7])
+    fetch_c = pltpu.make_async_copy(c_ref, c_near, local_sem.at[8])
+    fetch_o.start()
+    fetch_c.start()
     me.barrier()
 
     def rows_of(p):
@@ -214,15 +233,15 @@
     def head_slice(ref, p, width):
         return ref.at[:, :, pl.ds(pl.multiple_of(p * width, width), width)]
 
-    def over_peers(make, act):
+    def over_peers(make, act, across=False):
         def step(d, _):
             p = me.head_peer(d)
-            made = make(d, p, (me.ctx, p))
+            made = make(d, p, (me.across() if across else me.ctx, p))
             for copy in made if isinstance(made, list) else [made]:
                 act(copy)
             return 0
 
-        lax.fori_loop(1, nh, step, 0)
+        lax.fori_loop(0 if across else 1, nh, step, 0)
 
     def start(copy):
         copy.start()
@@ -236,35 +255,32 @@
     def wait_recv(copy):
         copy.wait_recv()
 
-    def kv_targets(i):
-        return kvd.at[i, me.ctx, own_rows], kvq.at[i, 1, own_rows]
-
-    def kv_copies(d, p, device):
-        cols = pl.ds(pl.multiple_of(p * HD, HD), HD)
-        return [
-            remote(
-                ref.at[j, :, cols],
-                kv_targets(i)[j],
+    kv_ref = (k_ref, v_ref)
+
+    def kv_target(i, j):
+        return kvq.at[i, 1, own_rows] if j else kvd.at[i, me.ctx, own_rows]
+
+    def kv_copies(i, j):
+        def made(d, p, device):
+            cols = pl.ds(pl.multiple_of(p * HD, HD), HD)
+            return remote(
+                kv_ref[i].at[j, :, cols],
+                kv_target(i, j),
                 kv_send.at[2 * i + j, d],
                 kv_recv.at[2 * i + j, d],
                 device,
             )
-            for i, ref in enumerate((k_ref, v_ref))
-            for j in range(2)
-        ]
-
-    def kv_arrivals(d, p, device):
-        return [
-            remote(
-                kv_targets(i)[j],
-                kv_targets(i)[j],
-                kv_send.at[2 * i + j, d],
-                kv_recv.at[2 * i + j, d],
-                device,
+
+        return made
+
+    def kx_copies(i):
+        def made(d, p, device):
+            cols = pl.ds(pl.multiple_of(p * HD, HD), HD)
+            return remote(
+                kv_ref[i].at[0, :, cols], kv_target(i, 0), kx_send.at[i, d], kx_recv.at[i, d], device
             )
-            for i in range(2)
-            for j in range(2)
-        ]
+
+        return made
 
     def q_copy(d, p, device):
         return remote(
@@ -279,75 +295,86 @@
     def d_copy(d, p, device):
         return remote(delta, d_in.at[:, me.h], d_send.at[d], d_recv.at[d], device)
 
-    over_peers(kv_copies, start)
-    over_peers(q_copy, start)
-    over_peers(c_copy, start)
-
+    for i in range(2):
+        over_peers(kv_copies(i, 0), start)
+        over_peers(kx_copies(i), start, True)
     own_cols = pl.ds(pl.multiple_of(me.h * HD, HD), HD)
     locals_ = [
-        pltpu.make_async_copy(ref.at[j, :, own_cols], kv_targets(i)[j], local_sem.at[2 * i + j])
-        for i, ref in enumerate((k_ref, v_ref))
+        pltpu.make_async_copy(kv_ref[i].at[j, :, own_cols], kv_target(i, j), local_sem.at[2 * i + j])
+        for i in range(2)
         for j in range(2)
     ]
     own_q = pltpu.make_async_copy(head_slice(q_ref, me.h, gw), q_in.at[:, me.h], local_sem.at[4])
     own_c = pltpu.make_async_copy(head_slice(c_ref, me.h, gw), c_in.at[:, me.h], local_sem.at[5])
     for copy in locals_:
         copy.start()
+    over_peers(q_copy, start)
+    for i in range(2):
+        over_peers(kv_copies(i, 1), start)
+    over_peers(c_copy, start)
     own_q.start()
     own_c.start()
-    for copy in locals_:
-        copy.wait()
-    over_peers(kv_arrivals, wait_recv)
-
-    def gather_copy(b, kind, device):
-        return remote(
-            kvd.at[:, b], kvd.at[:, b], g_send.at[kind, b], g_recv.at[b], device
-        )
-
-    sent = []
-
-    def send_block(b, kind, device):
-        copy = gather_copy(b, kind, device)
-        copy.start()
-        sent.append(copy)
-
-    def arrived(b):
-        gather_copy(b, 0, me.sibling()).wait_recv()
-
-    tail = pl.ds(bl - QMOST, QMOST)
-    tail_copy = remote(kvq.at[:, 1, tail], kvq.at[:, 0, tail], t_send, t_recv, me.ctx_next())
-
-    def gather_own(b):
-        send_block(b, 0, me.z_up())
-        send_block(b, 1, me.z_down())
-        send_block(b, 2, me.sibling())
-
-    def gather_step(q):
-        b = me.block_of(q, me.c)
-        arrived(b)
-        if me.far(q) < me.reach(q):
-            send_block(b, me.way(q), me.z_down() if me.way(q) == 0 else me.z_up())
-        send_block(b, 2, me.sibling())
-
-    send_block(me.ctx, 3, me.x_partner())
-    gather_own(me.ctx)
-    tail_copy.start()
-
+
+    fetch_o.wait()
+    fetch_c.wait()
     lanes = lax.broadcasted_iota(jnp.int32, (2, tok, HD), 2)
 
-    def one_head(j, acc):
-        at = pl.ds(pl.multiple_of(j * HD, HD), HD)
-        prod = c_ref[:, :, at].astype(jnp.float32) * o_ref[:, :, at].astype(jnp.float32)
-        return jnp.where(lanes == j, jnp.sum(prod, axis=-1, keepdims=True), acc)
-
-    delta[...] = lax.fori_loop(0, nhead, one_head, jnp.zeros((2, tok, HD), jnp.float32))
+    def some_heads(j, acc):
+        for u in range(UNROLL):
+            at = pl.ds(pl.multiple_of((j * UNROLL + u) * HD, HD), HD)
+            prod = c_near[:, :, at].astype(jnp.float32) * o_in[:, :, at].astype(jnp.float32)
+            part = jnp.sum(prod, axis=-1, keepdims=True)
+            acc = jnp.where(lanes == j * UNROLL + u, part, acc)
+        return acc
+
+    delta[...] = lax.fori_loop(
+        0, nhead // UNROLL, some_heads, jnp.zeros((2, tok, HD), jnp.float32)
+    )
     over_peers(d_copy, start)
     own_delta = pltpu.make_async_copy(delta, d_in.at[:, me.h], local_sem.at[6])
     own_delta.start()
 
-    other = me.block(1 - me.xh, me.z, me.c)
-    arrived(other)
-    gather_own(other)
+    def gather_copy(i, b, kind, device):
+        return remote(
+            kvd.at[i, b], kvd.at[i, b], g_send.at[i, kind, b], g_recv.at[i, b], device
+        )
+
+    sent = []
+
+    def send_block(i, b, kind, device):
+        copy = gather_copy(i, b, kind, device)
+        copy.start()
+        sent.append(copy)
+
+    def arrived(i, b):
+        gather_copy(i, b, 0, me.sibling()).wait_recv()
+
+    tail = pl.ds(bl - QMOST, QMOST)
+    tail_copy = remote(kvq.at[:, 1, tail], kvq.at[:, 0, tail], t_send, t_recv, me.ctx_next())
+
+    def gather_own(i, b):
+        send_block(i, b, 0, me.z_up())
+        send_block(i, b, 1, me.z_down())
+
+    def gather_step(f):
+        qs_at = [q for q in range(last - 1, 1, -1) if me.far(q) == f]
+        for i in range(2):
+            for q in qs_at:
+                b = me.block_of(q, me.c)
+                arrived(i, b)
+                if f < me.reach(q):
+                    way = me.way(q)
+                    send_block(i, b, way, me.z_down() if way == 0 else me.z_up())
+                send_block(i, b, 2, me.sibling())
+
+    for i in range(2):
+        locals_[2 * i].wait()
+        over_peers(kv_copies(i, 0), wait_recv)
+        gather_own(i, me.ctx)
+        over_peers(kx_copies(i), wait_recv, True)
+        gather_own(i, me.across())
+        send_block(i, me.ctx, 2, me.sibling())
+        send_block(i, me.across(), 2, me.sibling())
 
     count = len_ref.shape[1]
     lens = jnp.broadcast_to(len_ref[...].astype(jnp.float32), (8, count)).astype(jnp.bfloat16)
@@ -406,10 +433,12 @@
         def _():
             doc(doc_mask)
 
-    for q in range(4 * me.half - 1, 4 * me.half - 5, -1):
-        gather_step(q)
-    for q in range(4 * me.half - 5, max(4 * me.half - 9, 1), -1):
-        gather_step(q)
+    gather_step(1)
+    for i in range(2):
+        locals_[2 * i + 1].wait()
+        over_peers(kv_copies(i, 1), wait_recv)
+    tail_copy.start()
+    gather_step(2)
 
     own_q.wait()
     over_peers(q_copy, wait_recv)
@@ -421,7 +450,8 @@
     def peaks(first, count):
         def step(i, _):
             q = first - i
-            arrived(me.block_of(q, 1 - me.c))
+            for i in range(2):
+                arrived(i, me.block_of(q, 1 - me.c))
             t = me.pair_of(q)
             keys = doc_kv(0, t)
             on_pair(
@@ -436,11 +466,9 @@
     peak_sweep(1, question_kv(0), question_mask)
     peaks(last - 2, 4)
     for f in range(3, me.half + 1):
-        top = last - 2 - 4 * (f - 1)
-        for q in range(top, max(top - 4, 1), -1):
-            gather_step(q)
-        peaks(top + 4, 4)
-    peaks(3 if me.half > 1 else 1, 2)
+        gather_step(f)
+        peaks(last - 2 - 4 * (f - 2), 4)
+    peaks(3, 2)
 
     for s in range(2):
         final_max[s] = jnp.max(peak[s], axis=0, keepdims=True)
@@ -498,10 +526,11 @@
             me.sibling(),
         )
 
-    def hop_copy(way, xs, f):
+    def hop_copy(way, xs, f, wide):
+        source = sums if wide else low_sums
         return remote(
-            sums.at[me.pair(xs, me.z + f * (1 - 2 * way))],
-            chain.at[way, xs, f - 1],
+            source.at[me.pair(xs, me.z + f * (1 - 2 * way))],
+            chain.at[way, xs] if wide else low_chain.at[way, xs, f - 1],
             hop_send.at[way, xs, f - 1],
             hop_recv.at[way, xs, f - 1],
             me.dev(me.xh, me.z + 1 - 2 * way, me.c),
@@ -511,15 +540,26 @@
         f, way, xs, t = me.far(q), me.way(q), me.xs(q), me.pair_of(q)
         core_copy(t).wait_recv()
         sums[t] = dkv[t, :, me.c] + from_core[t]
-
-        @pl.when((f > 0) & (f < me.reach(q)))
+        met = (f > 0) & (f < me.reach(q))
+
+        @pl.when(met & (f + 1 == WIDE))
         def _():
-            hop_copy(way, xs, f + 1).wait_recv()
-            sums[t] = sums[t] + chain[way, xs, f]
-
-        @pl.when(f > 0)
+            hop_copy(way, xs, f + 1, True).wait_recv()
+            sums[t] = sums[t] + chain[way, xs]
+
+        @pl.when(met & (f + 1 != WIDE))
         def _():
-            hop_copy(way, xs, f).start()
+            hop_copy(way, xs, f + 1, False).wait_recv()
+            sums[t] = sums[t] + low_chain[way, xs, f].astype(jnp.float32)
+
+        @pl.when(f == WIDE)
+        def _():
+            hop_copy(way, xs, f, True).start()
+
+        @pl.when((f > 0) & (f != WIDE))
+        def _():
+            low_sums[t] = sums[t].astype(jnp.bfloat16)
+            hop_copy(way, xs, f, False).start()
 
     def backward_pair(n, _):
         q = n + 2
@@ -568,34 +608,46 @@
 
     lax.fori_loop(npair - LAG, npair, serve_rest, 0)
 
-    for way in range(2):
-        for xs in range(2):
-            hop_copy(way, xs, 1).wait_recv()
-    for xs in range(2):
-        t = me.pair(xs, me.z)
-        sums[t] = sums[t] + chain[0, xs, 0] + chain[1, xs, 0]
-    x_copy = remote(
-        sums.at[me.pair(1 - me.xh, me.z)], from_x, x_send, x_recv, me.x_partner()
-    )
-    x_copy.start()
     over_peers(out_copy, start)
     own_out.start()
     next_copy.wait_recv()
     for i in range(2):
         factor = SCALE if i == 0 else 1.0
-        result[i, 1, 0 : bl - QMOST] = dx[i, bl : 2 * bl - QMOST] * factor
-        result[i, 1, bl - QMOST : bl] = (
+        result[i, 0 : bl - QMOST] = dx[i, bl : 2 * bl - QMOST] * factor
+        result[i, bl - QMOST : bl] = (
             dx[i, 2 * bl - QMOST : 2 * bl] + from_next[i]
         ) * factor
 
-    def r_copies(s):
+    def r_copies(d, p, device):
+        return [
+            remote(
+                result.at[i, rows_of(p)],
+                (gk, gv)[i].at[1, :, own_cols],
+                r_send.at[i, d],
+                r_recv.at[i, d],
+                device,
+            )
+            for i in range(2)
+        ]
+
+    own_r = [
+        pltpu.make_async_copy(
+            result.at[i, own_rows], (gk, gv)[i].at[1, :, own_cols], local_sem.at[i]
+        )
+        for i in range(2)
+    ]
+    over_peers(r_copies, start)
+    for copy in own_r:
+        copy.start()
+
+    def final_copies(kind):
         def made(d, p, device):
             return [
                 remote(
-                    result.at[i, s, rows_of(p)],
-                    (gk, gv)[i].at[s, :, own_cols],
-                    r_send.at[2 * i + s, d],
-                    r_recv.at[2 * i + s, d],
+                    final.at[kind, i, rows_of(p)],
+                    landed.at[kind, i, me.h],
+                    f_send.at[kind, i, d],
+                    f_recv.at[kind, i, d],
                     device,
                 )
                 for i in range(2)
@@ -603,27 +655,43 @@
 
         return made
 
-    def own_r(i, s):
-        return pltpu.make_async_copy(
-            result.at[i, s, own_rows], (gk, gv)[i].at[s, :, own_cols], local_sem.at[2 * i + s]
-        )
-
-    over_peers(r_copies(1), start)
+    for way in range(2):
+        for xs in range(2):
+            hop_copy(way, xs, 1, False).wait_recv()
+    for kind in (1, 0):
+        xs = me.xh if kind == 0 else 1 - me.xh
+        t = me.pair(xs, me.z)
+        for i in range(2):
+            factor = SCALE if i == 0 else 1.0
+            final[kind, i] = (
+                sums[t, i]
+                + low_chain[0, xs, 0, i].astype(jnp.float32)
+                + low_chain[1, xs, 0, i].astype(jnp.float32)
+            ) * factor
+        over_peers(final_copies(kind), start, kind == 1)
     for i in range(2):
-        own_r(i, 1).start()
-    x_copy.wait_recv()
-    own = me.pair(me.xh, me.z)
+        landed[0, i, me.h] = final[0, i, own_rows]
+    over_peers(final_copies(0), wait_recv)
+    over_peers(final_copies(1), wait_recv, True)
     for i in range(2):
-        factor = SCALE if i == 0 else 1.0
-        result[i, 0] = (sums[own, i] + from_x[i]) * factor
-    over_peers(r_copies(0), start)
-    for i in range(2):
-        own_r(i, 0).start()
+        for h in range(nh):
+            owned[i, :, h * HD : (h + 1) * HD] = landed[0, i, h] + landed[1, i, h]
+    last_out = [
+        pltpu.make_async_copy(owned.at[i], (gk, gv)[i].at[0], local_sem.at[2 + i])
+        for i in range(2)
+    ]
+    for copy in last_out:
+        copy.start()
 
     for copy in sent:
         copy.wait_send()
-    for make in (kv_copies, q_copy, c_copy, d_copy):
+    for i in range(2):
+        over_peers(kx_copies(i), wait_send, True)
+        for j in range(2):
+            over_peers(kv_copies(i, j), wait_send)
+    for make in (q_copy, c_copy, d_copy, final_copies(0)):
         over_peers(make, wait_send)
+    over_peers(final_copies(1), wait_send, True)
     tail_copy.wait_send()
 
     def core_done(t, _):
@@ -634,15 +702,26 @@
     for way in range(2):
         for xs in range(2):
             for f in range(1, me.half + (way + xs) % 2):
-                hop_copy(way, xs, f).wait_send()
-    x_copy.wait_send()
+                hop_copy(way, xs, f, f == WIDE).wait_send()
     next_copy.wait_send()
-    for make in (out_copy, r_copies(0), r_copies(1)):
-        over_peers(make, wait)
+    over_peers(out_copy, wait)
+    over_peers(r_copies, wait)
     own_out.wait()
-    for i in range(2):
-        for s in range(2):
-            own_r(i, s).wait()
+    for copy in own_r + last_out:
+        copy.wait()
+
+
+def place_results(*refs):
+    sources, targets, held, sem = refs[:3], refs[3:6], refs[6:9], refs[9]
+    reads = [pltpu.make_async_copy(sources[i], held[i], sem.at[0, i]) for i in range(3)]
+    writes = [pltpu.make_async_copy(held[i], targets[i], sem.at[1, i]) for i in range(3)]
+    for copy in reads:
+        copy.start()
+    for i in range(3):
+        reads[i].wait()
+        writes[i].start()
+    for copy in writes:
+        copy.wait()
 
 
 def shards(queries, keys, values, outputs, cotangent, lengths):
@@ -661,14 +740,15 @@
     f32, b16 = jnp.float32, jnp.bfloat16
     shape = jax.ShapeDtypeStruct
     hops = nctx // 8
-    return pl.pallas_call(
+    made = (
+        shape((2, tok, nh * gw), b16),
+        shape((2, tok, nh * HD), f32),
+        shape((2, tok, nh * HD), f32),
+    )
+    results = pl.pallas_call(
         functools.partial(kernel, dims),
-        out_shape=(
-            shape((2, tok, nh * gw), b16),
-            shape((2, tok, nh * HD), f32),
-            shape((2, tok, nh * HD), f32),
-        ),
-        in_specs=[vmem, hbm, hbm, hbm, vmem, vmem],
+        out_shape=made,
+        in_specs=[vmem, hbm, hbm, hbm, hbm, hbm],
         out_specs=[hbm] * 3,
         scratch_shapes=[
             space((2, nh, tok, gw), b16),
@@ -694,20 +774,28 @@
             space((2, bl, gw), b16),
             space((npair, 2, bl, HD), f32),
             space((npair, 2, bl, HD), f32),
-            space((2, 2, hops, 2, bl, HD), f32),
+            space((npair, 2, bl, HD), b16),
+            space((2, 2, 2, bl, HD), f32),
+            space((2, 2, hops, 2, bl, HD), b16),
+            space((2, QMOST, HD), f32),
             space((2, bl, HD), f32),
-            space((2, QMOST, HD), f32),
             space((2, 2, bl, HD), f32),
+            space((2, 2, nh, tok, HD), f32),
+            space((2, tok, nh * HD), f32),
+            space((2, tok, nh * gw), b16),
+            space((2, tok, nh * gw), b16),
             dma((4, nh)),
             dma((4, nh)),
+            dma((2, nh)),
+            dma((2, nh)),
             dma((nh,)),
             dma((nh,)),
             dma((nh,)),
             dma((nh,)),
             dma((nh,)),
             dma((nh,)),
-            dma((4, nctx)),
-            dma((nctx,)),
+            dma((2, 3, nctx)),
+            dma((2, nctx)),
             dma,
             dma,
             dma((npair,)),
@@ -716,19 +804,27 @@
             dma((2, 2, hops)),
             dma,
             dma,
-            dma,
-            dma,
             dma((nh,)),
             dma((nh,)),
-            dma((4, nh)),
-            dma((4, nh)),
-            dma((7,)),
+            dma((2, nh)),
+            dma((2, nh)),
+            dma((2, 2, nh)),
+            dma((2, 2, nh)),
+            dma((9,)),
         ],
         compiler_params=pltpu.CompilerParams(
             collective_id=0, has_side_effects=True, vmem_limit_bytes=60 * 2**20
         ),
         name="attention_backward",
     )(lengths.reshape(1, -1), queries, keys, values, outputs, cotangent)
+    return pl.pallas_call(
+        place_results,
+        out_shape=made,
+        in_specs=[hbm] * 3,
+        out_specs=[hbm] * 3,
+        scratch_shapes=[space(m.shape, m.dtype) for m in made] + [dma((2, 3))],
+        name="place_results",
+    )(*results)
 
 
 def solution(mesh):

time: 105 us -> 93.1 us (0.89); the launches traced: 105 us -> 91.7 us
  Pallas kernels: 101 us -> 91 us
  local copies, waits for them, and re-layouts: 3.51 us -> 0 us
    pallas_call x1 -> x2, Pallas kernels: 101 us -> 91 us  [the longest x1 89.1 us: shards(): pl.pallas_call(functools.partial(kernel, dims), out_shape=made, in_specs=...]
    unnamed x7 -> x0, local copies, waits for them, and re-layouts: 3.51 us -> none
where the time goes in v3:
time: 93.1 us; the launch traced here: 91.7 us
  Pallas kernels  91 us (98%)
    pallas_call x1, Pallas kernels, shards(): pl.pallas_call(functools.partial(kernel, dims), out_shape=made, in_specs=...  89.1 us
    pallas_call x1, Pallas kernels, shards(): pl.pallas_call(place_results, out_shape=made, in_specs=[hbm] * 3, out_spe...  1.96 us

profile of v3, /device:TPU:4, one launch (start us, length us, event | category | flops | bytes accessed | tf_op | source)
XLA Modules:
  0.0 91.7 jit_solution(15979511795524340690)
XLA Ops:
  0.6 89.1 %attention_backward.1 = (bf16[2,16,8192]{2,1,0:T(8,128)(2,1)}, f32[2,16,1024]{2,1,0:T(8,128)}, f32[2,16,1024]{2,1,0:T(8,128)}) custom-call(s32[1,256]{1,0:T(1,128)} %bitcast.1, bf16[2,16,8192]{2,1,0:T(8,128)(2,1)} %q_ref.1, bf16[2,16,1024]{2,1,0:T(8,128)(2,1)} %k_ref.1, bf16[2,16,1024]{2,1,0:T(8,128)(2,1)} %v_ref.1, bf16[2,16,8192]{2,1,0:T(8,128)(2,1)} %o_ref.1, ...), custom_call_target="tpu_custom_call" | custom-call | tf_op jit(solution)/shard_map/attention_backward/pallas_call | solution.py:748
  89.7 2.0 %place_results.1 = (bf16[2,16,8192]{2,1,0:T(8,128)(2,1)}, f32[2,16,1024]{2,1,0:T(8,128)}, f32[2,16,1024]{2,1,0:T(8,128)}) custom-call(bf16[2,16,8192]{2,1,0:T(8,128)(2,1)} %get-tuple-element.6.refs_0_, f32[2,16,1024]{2,1,0:T(8,128)} %get-tuple-element.7.refs_1_, f32[2,16,1024]{2,1,0:T(8,128)} %get-tuple-element.8.refs_2_), custom_call_target="tpu_custom_call" | custom-call | tf_op jit(solution)/shard_map/place_results/pallas_call | solution.py:820

commit v4 on v3

v4 whole, which is shorter than its diff:
```python
import functools
import math

import jax
import jax.numpy as jnp
from jax import lax
from jax.experimental import pallas as pl
from jax.experimental.pallas import tpu as pltpu
from jax.sharding import PartitionSpec as P

HD = 128
NEG_FILL = -1e30
QMOST = 32
SCALE = HD ** (-0.5)
EXP2_SCALE = SCALE * math.log2(math.e)
MESH = pl.DeviceIdType.MESH
LAG = 2
UNROLL = 4


def remote(src, dst, send_sem, recv_sem, device):
    return pltpu.make_async_remote_copy(
        src_ref=src,
        dst_ref=dst,
        send_sem=send_sem,
        recv_sem=recv_sem,
        device_id=device,
        device_id_type=MESH,
    )


class Place:
    def __init__(self, ctx_count, head_count):
        self.nctx = ctx_count
        self.nh = head_count
        self.nz = ctx_count // 4
        self.half = self.nz // 2
        self.npair = ctx_count // 2
        self.ctx = lax.axis_index("ctx")
        self.h = lax.axis_index("head")
        self.c = lax.rem(self.ctx, 2)
        self.z = lax.rem(self.ctx // 2, self.nz)
        self.xh = self.ctx // (2 * self.nz)

    def zmod(self, z):
        return lax.rem(z + self.nz, self.nz)

    def block(self, xh, z, c):
        return (xh * self.nz + self.zmod(z)) * 2 + c

    def pair(self, xh, z):
        return xh * self.nz + self.zmod(z)

    def dev(self, xh, z, c):
        return (self.block(xh, z, c), self.h)

    def z_up(self):
        return self.dev(self.xh, self.z + 1, self.c)

    def z_down(self):
        return self.dev(self.xh, self.z - 1, self.c)

    def across(self):
        return self.block(1 - self.xh, self.z, self.c)

    def sibling(self):
        return self.dev(self.xh, self.z, 1 - self.c)

    def ctx_next(self):
        return (lax.rem(self.ctx + 1, self.nctx), self.h)

    def ctx_prev(self):
        return (lax.rem(self.ctx + self.nctx - 1, self.nctx), self.h)

    def head_peer(self, d):
        return lax.rem(self.h + d, self.nh)

    def far(self, q):
        return self.half - q // 4

    def way(self, q):
        return q % 2

    def xs(self, q):
        return (q // 2 + q) % 2

    def reach(self, q):
        return self.half - (self.way(q) + self.xs(q) + 1) % 2

    def z_of(self, q):
        return self.z + self.far(q) * (1 - 2 * self.way(q))

    def pair_of(self, q):
        return self.pair(self.xs(q), self.z_of(q))

    def block_of(self, q, c):
        return self.block(self.xs(q), self.z_of(q), c)

    def barrier(self):
        barrier = pltpu.get_barrier_semaphore()

        def greet(d, _):
            pl.semaphore_signal(
                barrier, inc=1, device_id=(self.ctx, self.head_peer(d)), device_id_type=MESH
            )
            return 0

        def greet_across(d, _):
            device = (self.across(), self.head_peer(d))
            pl.semaphore_signal(barrier, inc=1, device_id=device, device_id_type=MESH)
            return 0

        lax.fori_loop(1, self.nh, greet, 0)
        lax.fori_loop(0, self.nh, greet_across, 0)
        near = (
            self.z_up(),
            self.z_down(),
            self.sibling(),
            self.ctx_next(),
            self.ctx_prev(),
        )
        for device in near:
            pl.semaphore_signal(barrier, inc=1, device_id=device, device_id_type=MESH)
        pl.semaphore_wait(barrier, 2 * self.nh - 1 + len(near))


def nt_dot(a, b):
    return lax.dot_general(a, b, (((1,), (1,)), ((), ())), preferred_element_type=jnp.float32)


def nn_dot(a, b):
    return jnp.dot(a, b, preferred_element_type=jnp.float32)


def by_sublane(x):
    return x.reshape(x.shape[0] // 8, 8, x.shape[1])


def kernel(
    dims,
    len_ref,
    q_ref,
    k_ref,
    v_ref,
    o_ref,
    c_ref,
    gq,
    gk,
    gv,
    q_in,
    c_in,
    d_in,
    kvd,
    kvq,
    delta,
    delta_t,
    qs,
    cs,
    dd,
    turn,
    weights,
    peak,
    total,
    first_max,
    final_max,
    inverse,
    dqt,
    keys_t,
    low_p,
    low_s,
    dkv,
    dx,
    dq,
    from_core,
    sums,
    low_sums,
    chain,
    from_next,
    result,
    final,
    landed,
    owned,
    o_in,
    c_near,
    kv_send,
    kv_recv,
    q_send,
    q_recv,
    c_send,
    c_recv,
    d_send,
    d_recv,
    g_send,
    g_recv,
    s_send,
    s_recv,
    t_send,
    t_recv,
    core_send,
    core_recv,
    hop_send,
    hop_recv,
    n_send,
    n_recv,
    o_send,
    o_recv,
    r_send,
    r_recv,
    f_send,
    f_recv,
    local_sem,
):
    nctx, nh, tok, gw, bl, nhead = dims
    me = Place(nctx, nh)
    npair = me.npair
    last = 4 * me.half + 1
    group = gw // HD
    rows = group * bl
    tile = 2 * bl
    own_pair = me.ctx // 2
    chunk = min(256, rows)
    every = [pl.ds(r * chunk, chunk) for r in range(rows // chunk)]
    fetch_o = pltpu.make_async_copy(o_ref, o_in, local_sem.at[7])
    fetch_c = pltpu.make_async_copy(c_ref, c_near, local_sem.at[8])
    fetch_o.start()
    fetch_c.start()
    me.barrier()

    def rows_of(p):
        return pl.ds(pl.multiple_of(p * tok, tok), tok)

    own_rows = rows_of(me.h)

    def over_peers(make, act, across=False):
        def step(d, _):
            p = me.head_peer(d)
            made = make(d, p, (me.across() if across else me.ctx, p))
            for copy in made if isinstance(made, list) else [made]:
                act(copy)
            return 0

        lax.fori_loop(0 if across else 1, nh, step, 0)

    def sent_all(like, sem):
        remote(like, like, sem, sem, me.sibling()).wait_send()

    def received_all(like, sem):
        remote(like, like, sem, sem, me.sibling()).wait_recv()

    peers = nh - 1
    peer_rows = pl.ds(0, peers * tok)

    def start(copy):
        copy.start()

    kv_ref = (k_ref, v_ref)

    def kv_target(i, j):
        return kvq.at[i, 1, own_rows] if j else kvd.at[i, me.ctx, own_rows]

    def kv_copies(i, j):
        def made(d, p, device):
            cols = pl.ds(pl.multiple_of(p * HD, HD), HD)
            return remote(
                kv_ref[i].at[j, :, cols],
                kv_target(i, j),
                kv_send.at[i, j],
                kv_recv.at[i, j],
                device,
            )

        return made

    def kx_copies(i):
        def made(d, p, device):
            cols = pl.ds(pl.multiple_of(p * HD, HD), HD)
            return remote(
                kv_ref[i].at[0, :, cols], kv_target(i, 0), kv_send.at[i, 2], kv_recv.at[i, 2], device
            )

        return made

    def head_part(kind, ref, p):
        return ref.at[1 - kind, :, pl.ds(pl.multiple_of(p * gw, gw), gw)]

    def place_of(kind, ref):
        return ref.at[1 - kind, me.h]

    def row_copies(kind, source, target, send, recv):
        def made(d, p, device):
            return remote(
                head_part(kind, source, p),
                place_of(kind, target),
                send.at[kind],
                recv.at[kind],
                device,
            )

        return made

    def q_copies(kind):
        return row_copies(kind, q_ref, q_in, q_send, q_recv)

    def c_copies(kind):
        return row_copies(kind, c_ref, c_in, c_send, c_recv)

    def over_rows(copies, act):
        for kind in range(2):
            over_peers(copies(kind), act)

    def d_copy(d, p, device):
        return remote(
            delta_t.at[pl.ds(pl.multiple_of(p * group, group), group)],
            d_in.at[me.h],
            d_send,
            d_recv,
            device,
        )

    for i in range(2):
        over_peers(kv_copies(i, 0), start)
        over_peers(kx_copies(i), start, True)
    own_cols = pl.ds(pl.multiple_of(me.h * HD, HD), HD)
    locals_ = [
        pltpu.make_async_copy(kv_ref[i].at[j, :, own_cols], kv_target(i, j), local_sem.at[2 * i + j])
        for i in range(2)
        for j in range(2)
    ]
    own_q = [
        pltpu.make_async_copy(head_part(k, q_ref, me.h), place_of(k, q_in), local_sem.at[4 + k])
        for k in range(2)
    ]
    own_c = [
        pltpu.make_async_copy(head_part(k, c_ref, me.h), place_of(k, c_in), local_sem.at[9 + k])
        for k in range(2)
    ]
    for copy in locals_:
        copy.start()
    over_rows(q_copies, start)
    for i in range(2):
        over_peers(kv_copies(i, 1), start)
    for copy in own_q + own_c:
        copy.start()

    fetch_o.wait()
    fetch_c.wait()
    lanes = lax.broadcasted_iota(jnp.int32, (2, tok, HD), 2)

    def some_heads(j, acc):
        for u in range(UNROLL):
            at = pl.ds(pl.multiple_of((j * UNROLL + u) * HD, HD), HD)
            prod = c_near[:, :, at].astype(jnp.float32) * o_in[:, :, at].astype(jnp.float32)
            part = jnp.sum(prod, axis=-1, keepdims=True)
            acc = jnp.where(lanes == j * UNROLL + u, part, acc)
        return acc

    delta[...] = lax.fori_loop(
        0, nhead // UNROLL, some_heads, jnp.zeros((2, tok, HD), jnp.float32)
    )
    delta_t[:, 0 : 2 * tok] = jnp.transpose(delta[...].reshape(2 * tok, HD))
    over_peers(d_copy, start)
    d_in[me.h] = delta_t[pl.ds(pl.multiple_of(me.h * group, group), group)]

    n_sent = {"ring": 0, "core": 0}

    def ring_copy(i, b, f, way, xs, device):
        return remote(kvd.at[i, b], kvd.at[i, b], g_send, g_recv.at[i, f - 1, way, xs], device)

    def ring_send(i, b, f, way, xs):
        ring_copy(i, b, f, way, xs, me.z_down() if way == 0 else me.z_up()).start()
        n_sent["ring"] += 1

    def core_send_block(i, b, f):
        sem = s_recv.at[f if i == 0 else me.half + 1]
        remote(kvd.at[i, b], kvd.at[i, b], s_send, sem, me.sibling()).start()
        n_sent["core"] += 1

    tail = pl.ds(bl - QMOST, QMOST)
    tail_copy = remote(kvq.at[:, 1, tail], kvq.at[:, 0, tail], t_send, t_recv, me.ctx_next())

    def gather_own(i, b, xs):
        ring_send(i, b, 1, 1, xs)
        ring_send(i, b, 1, 0, xs)

    def gather_step(f, kv=(0, 1)):
        qs_at = [q for q in range(last - 1, 1, -1) if me.far(q) == f]
        for i in kv:
            for q in qs_at:
                b, way, xs = me.block_of(q, me.c), me.way(q), me.xs(q)
                ring_copy(i, b, f, way, xs, me.sibling()).wait_recv()
                if f < me.reach(q):
                    ring_send(i, b, f + 1, way, xs)
                core_send_block(i, b, f)

    for i in range(2):
        locals_[2 * i].wait()
        received_all(kvd.at[i, me.ctx, peer_rows], kv_recv.at[i, 0])
        gather_own(i, me.ctx, me.xh)
        received_all(kvd.at[i, me.across()], kv_recv.at[i, 2])
        gather_own(i, me.across(), 1 - me.xh)
        core_send_block(i, me.ctx, 0)
        core_send_block(i, me.across(), 0)

    count = len_ref.shape[1]
    lens = jnp.broadcast_to(len_ref[...].astype(jnp.float32), (8, count)).astype(jnp.bfloat16)
    i0 = lax.broadcasted_iota(jnp.int32, (count, count), 0)
    i1 = lax.broadcasted_iota(jnp.int32, (count, count), 1)
    before = jnp.where(i0 < i1, 1.0, 0.0).astype(jnp.bfloat16)
    after = jnp.where(i1 < i0, 1.0, 0.0).astype(jnp.bfloat16)
    starts_row = nn_dot(lens, before)[0:1, :]
    starts_col = nt_dot(after, lens)[:, 0:1]
    row_at = lax.broadcasted_iota(jnp.int32, (1, chunk), 1) % bl
    key_at = lax.broadcasted_iota(jnp.int32, (tile, 1), 0) - bl
    row_off = (row_at + me.ctx * bl).astype(jnp.float32)
    key_off = (key_at + me.ctx * bl).astype(jnp.float32)
    row_seg = jnp.sum(jnp.where(starts_col <= row_off, 1.0, 0.0), axis=0, keepdims=True)
    key_seg = jnp.sum(jnp.where(starts_row <= key_off, 1.0, 0.0), axis=1, keepdims=True)
    question_mask = (key_at <= row_at) & (key_seg == row_seg)
    doc_key = lax.broadcasted_iota(jnp.int32, (tile, 1), 0) + (own_pair * 2 - me.ctx) * bl
    doc_mask = doc_key <= row_at

    peak[...] = jnp.full(peak.shape, NEG_FILL, jnp.float32)
    total[...] = jnp.zeros(total.shape, jnp.float32)
    dqt[...] = jnp.zeros(dqt.shape, jnp.float32)

    def doc_kv(i, t):
        return kvd[i, pl.ds(2 * t, 2)].reshape(tile, HD)

    def question_kv(i):
        at = lax.broadcasted_iota(jnp.int32, (bl, HD), 0)
        prev = jnp.where(at >= bl - QMOST, kvq[i, 0].astype(jnp.float32), 0.0)
        return jnp.concatenate([prev.astype(jnp.bfloat16), kvq[i, 1]], axis=0)

    def scores_of(s, keys, mask, cols):
        scores = nt_dot(keys, qs[s, cols, :])
        return scores if mask is None else jnp.where(mask, scores, NEG_FILL)

    def peak_sweep(s, keys, mask, at):
        for cols in at:
            scores = by_sublane(scores_of(s, keys, mask, cols))
            peak[s, :, cols] = jnp.maximum(peak[s, :, cols], jnp.max(scores, axis=0))

    def weight_sweep(s, slot, keys, mask, at, known):
        for cols in at:
            scores = scores_of(s, keys, mask, cols)
            part = jnp.exp2((scores - known[s, 0:1, cols]) * EXP2_SCALE)
            weights[slot, :, cols] = part
            total[s, :, cols] = total[s, :, cols] + jnp.sum(by_sublane(part), axis=0)

    def on_pair(t, sweep):
        sweep(1, None, every)

        @pl.when(t < own_pair)
        def _():
            sweep(0, None, every)

        @pl.when(t == own_pair)
        def _():
            sweep(0, doc_mask, every)

    def sort_rows(target, source, s):
        for g in range(group):
            cols = slice(g * HD, (g + 1) * HD)
            target[s, g * bl : (g + 1) * bl, :] = source[s, :, :, cols].reshape(bl, HD)

    def peaks(f):
        count = 4 if 0 < f < me.half else 2
        received_all(kvd.at[0, pl.ds(0, count)], s_recv.at[f])

        def step(i, _):
            q = last - i if f == 0 else last - 2 - 4 * (f - 1) - i
            t = me.pair_of(q)
            keys = doc_kv(0, t)

            def sweep(s, mask, at):
                peak_sweep(s, keys, mask, at)

            on_pair(t, sweep)
            return 0

        lax.fori_loop(0, count, step, 0)

    def weigh(low, high, known):
        def step(q, _):
            t = me.pair_of(q)
            keys = doc_kv(0, t)

            def sweep(s, mask, at):
                weight_sweep(s, s * npair + t, keys, mask, at, known)

            on_pair(t, sweep)
            return 0

        lax.fori_loop(low, high, step, 0)

    gather_step(1)
    for i in range(2):
        locals_[2 * i + 1].wait()
        received_all(kvq.at[i, 1, peer_rows], kv_recv.at[i, 1])
    tail_copy.start()
    gather_step(2)
    for copy in own_q:
        copy.wait()
    for kind in range(2):
        received_all(q_in.at[kind, pl.ds(0, peers)], q_recv.at[kind])
    over_rows(c_copies, start)
    for s in range(2):
        sort_rows(qs, q_in, s)

    peaks(0)
    tail_copy.wait_recv()
    peak_sweep(1, question_kv(0), question_mask, every)
    for f in range(1, me.half - 1):
        if f + 1 > 2:
            gather_step(f + 1)
        peaks(f)
    for s in range(2):
        first_max[s] = jnp.max(peak[s], axis=0, keepdims=True)
    weight_sweep(1, 2 * npair, question_kv(0), question_mask, every, first_max)
    near = max(8, 4 * me.half - 4)
    weigh(near, last + 1, first_max)
    if me.half > 2:
        gather_step(me.half, (0,))
    weigh(8, near, first_max)
    if me.half > 2:
        gather_step(me.half, (1,))
    peaks(me.half - 1)
    peaks(me.half)
    for s in range(2):
        final_max[s] = jnp.max(peak[s], axis=0, keepdims=True)
        total[s] = total[s] * jnp.exp2((first_max[s] - final_max[s]) * EXP2_SCALE)
    weigh(2, 8, final_max)
    for s in range(2):
        whole = 1.0 / jnp.sum(total[s], axis=0, keepdims=True)
        nearer = whole * jnp.exp2((first_max[s] - final_max[s]) * EXP2_SCALE)
        inverse[0, s] = whole
        inverse[1, s] = nearer
        inverse[2, s] = nearer

    received_all(kvd.at[1, pl.ds(0, npair)], s_recv.at[me.half + 1])

    for copy in own_c:
        copy.wait()
    for kind in range(2):
        received_all(c_in.at[kind, pl.ds(0, peers)], c_recv.at[kind])
    received_all(d_in.at[pl.ds(0, peers)], d_recv)
    for s in range(2):
        sort_rows(cs, c_in, s)
        for j in range(nh):
            turn[:, j * tok : (j + 1) * tok] = d_in[j, :, s * tok : (s + 1) * tok]
        for g in range(group):
            dd[s, 0:1, g * bl : (g + 1) * bl] = turn[g : g + 1, :]

    def backward(s, slot, values, scale_at):
        for cols in every:
            prob = weights[slot, :, cols] * inverse[scale_at, s, 0:1, cols]
            d_prob = nt_dot(values, cs[s, cols, :])
            low_p[:, cols] = prob.astype(jnp.bfloat16)
            low_s[:, cols] = (prob * (d_prob - dd[s, 0:1, cols])).astype(jnp.bfloat16)
        d_value = nn_dot(low_p[...], cs[s])
        d_key = nn_dot(low_s[...], qs[s])
        dqt[s] += nn_dot(keys_t[...], low_s[...])
        return d_key, d_value

    def turn_keys(keys):
        keys_t[...] = jnp.transpose(keys.astype(jnp.float32)).astype(jnp.bfloat16)

    def put(t, i, value, add):
        for c in range(2):
            part = value[c * bl : (c + 1) * bl]
            dkv[t, i, c] = dkv[t, i, c] + part if add else part

    def core_copy(t):
        return remote(
            dkv.at[t, :, 1 - me.c],
            from_core.at[t],
            core_send,
            core_recv.at[t],
            me.sibling(),
        )

    def hop_copy(way, xs, f):
        return remote(
            low_sums.at[me.pair(xs, me.z + f * (1 - 2 * way))],
            chain.at[way, xs, f - 1],
            hop_send,
            hop_recv.at[way, xs, f - 1],
            me.dev(me.xh, me.z + 1 - 2 * way, me.c),
        )

    def serve(q):
        f, way, xs, t = me.far(q), me.way(q), me.xs(q), me.pair_of(q)
        core_copy(t).wait_recv()
        sums[t] = dkv[t, :, me.c] + from_core[t]

        @pl.when((f > 0) & (f < me.reach(q)))
        def _():
            hop_copy(way, xs, f + 1).wait_recv()
            sums[t] = sums[t] + chain[way, xs, f].astype(jnp.float32)

        @pl.when(f > 0)
        def _():
            low_sums[t] = sums[t].astype(jnp.bfloat16)
            hop_copy(way, xs, f).start()

    turn_keys(question_kv(0))
    dx[0], dx[1] = backward(1, 2 * npair, question_kv(1), 1)
    next_copy = remote(dx.at[:, tail], from_next, n_send, n_recv, me.ctx_prev())
    next_copy.start()

    def r_copies(d, p, device):
        return [
            remote(
                result.at[i, rows_of(p)],
                (gk, gv)[i].at[1, :, own_cols],
                r_send.at[i],
                r_recv.at[i],
                device,
            )
            for i in range(2)
        ]

    own_r = [
        pltpu.make_async_copy(
            result.at[i, own_rows], (gk, gv)[i].at[1, :, own_cols], local_sem.at[i]
        )
        for i in range(2)
    ]

    def send_questions():
        next_copy.wait_recv()
        for i in range(2):
            factor = SCALE if i == 0 else 1.0
            result[i, 0 : bl - QMOST] = dx[i, bl : 2 * bl - QMOST] * factor
            result[i, bl - QMOST : bl] = (
                dx[i, 2 * bl - QMOST : 2 * bl] + from_next[i]
            ) * factor
        over_peers(r_copies, start)
        for copy in own_r:
            copy.start()

    def backward_pair(n, _):
        q = n + 2
        t = me.pair_of(q)
        turn_keys(doc_kv(0, t))
        for i, value in enumerate(backward(1, npair + t, doc_kv(1, t), q // 8)):
            put(t, i, value, False)

        @pl.when(t <= own_pair)
        def _():
            for i, value in enumerate(backward(0, t, doc_kv(1, t), q // 8)):
                put(t, i, value, True)

        core_copy(t).start()

        @pl.when(n >= LAG)
        def _():
            serve(q - LAG)

        @pl.when(n == npair // 2)
        def _():
            send_questions()

        return 0

    lax.fori_loop(0, npair, backward_pair, 0)

    for s in range(2):
        for g in range(group):
            part = jnp.transpose(dqt[s, :, g * bl : (g + 1) * bl])
            dq[s, :, g * HD : (g + 1) * HD] = (part * SCALE).astype(jnp.bfloat16)

    def out_part(kind, p):
        return dq.at[1 - kind, rows_of(p)]

    def out_copies(kind):
        def made(d, p, device):
            return remote(
                out_part(kind, p),
                head_part(kind, gq, me.h),
                o_send.at[kind],
                o_recv.at[kind],
                device,
            )

        return made

    own_out = [
        pltpu.make_async_copy(out_part(k, me.h), head_part(k, gq, me.h), local_sem.at[4 + k])
        for k in range(2)
    ]
    over_rows(out_copies, start)
    for copy in own_out:
        copy.start()

    def serve_rest(n, _):
        serve(n + 2)
        return 0

    lax.fori_loop(npair - LAG, npair, serve_rest, 0)

    def final_copies(kind):
        def made(d, p, device):
            return [
                remote(
                    final.at[kind, i, rows_of(p)],
                    landed.at[kind, i, me.h],
                    f_send.at[kind, i],
                    f_recv.at[kind, i],
                    device,
                )
                for i in range(2)
            ]

        return made

    for way in range(2):
        for xs in range(2):
            hop_copy(way, xs, 1).wait_recv()
    for kind in (1, 0):
        xs = me.xh if kind == 0 else 1 - me.xh
        t = me.pair(xs, me.z)
        for i in range(2):
            factor = SCALE if i == 0 else 1.0
            final[kind, i] = (
                sums[t, i]
                + chain[0, xs, 0, i].astype(jnp.float32)
                + chain[1, xs, 0, i].astype(jnp.float32)
            ) * factor
        over_peers(final_copies(kind), start, kind == 1)
    for i in range(2):
        landed[0, i, me.h] = final[0, i, own_rows]
    for i in range(2):
        received_all(landed.at[0, i, pl.ds(0, peers)], f_recv.at[0, i])
        received_all(landed.at[1, i], f_recv.at[1, i])
    for i in range(2):
        for h in range(nh):
            owned[i, :, h * HD : (h + 1) * HD] = landed[0, i, h] + landed[1, i, h]
    last_out = [
        pltpu.make_async_copy(owned.at[i], (gk, gv)[i].at[0], local_sem.at[2 + i])
        for i in range(2)
    ]
    for copy in last_out:
        copy.start()

    sent_all(kvd.at[0, pl.ds(0, n_sent["ring"])], g_send)
    sent_all(kvd.at[0, pl.ds(0, n_sent["core"])], s_send)
    for i in range(2):
        sent_all(kvd.at[i, 0, peer_rows], kv_send.at[i, 0])
        sent_all(kvd.at[i, 0, peer_rows], kv_send.at[i, 1])
        sent_all(kvd.at[i, 0], kv_send.at[i, 2])
        sent_all(result.at[i, peer_rows], r_send.at[i])
        sent_all(final.at[0, i, peer_rows], f_send.at[0, i])
        sent_all(final.at[1, i], f_send.at[1, i])
        sent_all(q_in.at[i, pl.ds(0, peers)], q_send.at[i])
        sent_all(c_in.at[i, pl.ds(0, peers)], c_send.at[i])
        sent_all(dq.at[i, peer_rows], o_send.at[i])
        received_all(dq.at[i, peer_rows], o_recv.at[i])
        received_all(result.at[i, peer_rows], r_recv.at[i])
    sent_all(d_in.at[pl.ds(0, peers)], d_send)
    tail_copy.wait_send()
    sent_all(from_core, core_send)
    sent_all(low_sums.at[pl.ds(0, 4 * me.half - 2)], hop_send)
    next_copy.wait_send()
    for copy in own_out + own_r + last_out:
        copy.wait()


def place_results(*refs):
    sources, targets, held, sem = refs[:3], refs[3:6], refs[6:9], refs[9]
    reads = [pltpu.make_async_copy(sources[i], held[i], sem.at[0, i]) for i in range(3)]
    writes = [pltpu.make_async_copy(held[i], targets[i], sem.at[1, i]) for i in range(3)]
    for copy in reads:
        copy.start()
    for i in range(3):
        reads[i].wait()
        writes[i].start()
    for copy in writes:
        copy.wait()


def shards(queries, keys, values, outputs, cotangent, lengths):
    nctx, nh = lax.axis_size("ctx"), lax.axis_size("head")
    tok = queries.shape[1]
    gw = queries.shape[2] // nh
    bl = tok * nh
    nhead = queries.shape[2] // HD
    dims = (nctx, nh, tok, gw, bl, nhead)
    npair = nctx // 2
    group = gw // HD
    rows = group * bl
    hbm = pl.BlockSpec(memory_space=pl.ANY)
    vmem = pl.BlockSpec(memory_space=pltpu.VMEM)
    dma = pltpu.SemaphoreType.DMA
    space = pltpu.VMEM
    f32, b16 = jnp.float32, jnp.bfloat16
    shape = jax.ShapeDtypeStruct
    hops = nctx // 8
    made = (
        shape((2, tok, nh * gw), b16),
        shape((2, tok, nh * HD), f32),
        shape((2, tok, nh * HD), f32),
    )
    results = pl.pallas_call(
        functools.partial(kernel, dims),
        out_shape=made,
        in_specs=[vmem, hbm, hbm, hbm, hbm, hbm],
        out_specs=[hbm] * 3,
        scratch_shapes=[
            space((2, nh, tok, gw), b16),
            space((2, nh, tok, gw), b16),
            space((nh, group, HD), f32),
            space((2, nctx, bl, HD), b16),
            space((2, 2, bl, HD), b16),
            space((2, tok, HD), f32),
            space((HD, HD), f32),
            space((2, rows, HD), b16),
            space((2, rows, HD), b16),
            space((2, 1, rows), f32),
            space((group, bl), f32),
            space((2 * npair + 1, 2 * bl, rows), f32),
            space((2, 8, rows), f32),
            space((2, 8, rows), f32),
            space((2, 1, rows), f32),
            space((2, 1, rows), f32),
            space((3, 2, 1, rows), f32),
            space((2, HD, rows), f32),
            space((HD, 2 * bl), b16),
            space((2 * bl, rows), b16),
            space((2 * bl, rows), b16),
            space((npair, 2, 2, bl, HD), f32),
            space((2, 2 * bl, HD), f32),
            space((2, bl, gw), b16),
            space((npair, 2, bl, HD), f32),
            space((npair, 2, bl, HD), f32),
            space((npair, 2, bl, HD), b16),
            space((2, 2, hops, 2, bl, HD), b16),
            space((2, QMOST, HD), f32),
            space((2, bl, HD), f32),
            space((2, 2, bl, HD), f32),
            space((2, 2, nh, tok, HD), f32),
            space((2, tok, nh * HD), f32),
            space((2, tok, nh * gw), b16),
            space((2, tok, nh * gw), b16),
            dma((2, 3)),
            dma((2, 3)),
            dma((2,)),
            dma((2,)),
            dma((2,)),
            dma((2,)),
            dma,
            dma,
            dma,
            dma((2, hops, 2, 2)),
            dma,
            dma((hops + 2,)),
            dma,
            dma,
            dma,
            dma((npair,)),
            dma,
            dma((2, 2, hops)),
            dma,
            dma,
            dma((2,)),
            dma((2,)),
            dma((2,)),
            dma((2,)),
            dma((2, 2)),
            dma((2, 2)),
            dma((11,)),
        ],
        compiler_params=pltpu.CompilerParams(
            collective_id=0, has_side_effects=True, vmem_limit_bytes=60 * 2**20
        ),
        name="attention_backward",
    )(lengths.reshape(1, -1), queries, keys, values, outputs, cotangent)
    return pl.pallas_call(
        place_results,
        out_shape=made,
        in_specs=[hbm] * 3,
        out_specs=[hbm] * 3,
        scratch_shapes=[space(m.shape, m.dtype) for m in made] + [dma((2, 3))],
        name="place_results",
    )(*results)


def solution(mesh):
    spec = P(None, ("ctx", "head"), None)
    return jax.shard_map(
        shards,
        mesh=mesh,
        in_specs=(spec,) * 5 + (P(),),
        out_specs=(spec,) * 3,
        check_vma=False,
    )
```

time: 93.1 us -> 82.7 us (0.89)
  Pallas kernels: 91 us -> 81.4 us
    pallas_call x1, Pallas kernels: 89.1 us -> 79.4 us  [shards(): pl.pallas_call(functools.partial(kernel, dims), out_shape=made, in_specs=...]
where the time goes in v4:
time: 82.7 us; the launch traced here: 82 us
  Pallas kernels  81.4 us (98%)
    pallas_call x1, Pallas kernels, shards(): pl.pallas_call(functools.partial(kernel, dims), out_shape=made, in_specs=...  79.4 us
    pallas_call x1, Pallas kernels, shards(): pl.pallas_call(place_results, out_shape=made, in_specs=[hbm] * 3, out_spe...  1.96 us

profile of v4, /device:TPU:4, one launch (start us, length us, event | category | flops | bytes accessed | tf_op | source)
XLA Modules:
  0.0 82.0 jit_solution(16686219128909939290)
XLA Ops:
  0.6 79.4 %attention_backward.1 = (bf16[2,16,8192]{2,1,0:T(8,128)(2,1)}, f32[2,16,1024]{2,1,0:T(8,128)}, f32[2,16,1024]{2,1,0:T(8,128)}) custom-call(s32[1,256]{1,0:T(1,128)} %bitcast.1, bf16[2,16,8192]{2,1,0:T(8,128)(2,1)} %q_ref.1, bf16[2,16,1024]{2,1,0:T(8,128)(2,1)} %k_ref.1, bf16[2,16,1024]{2,1,0:T(8,128)(2,1)} %v_ref.1, bf16[2,16,8192]{2,1,0:T(8,128)(2,1)} %o_ref.1, ...), custom_call_target="tpu_custom_call" | custom-call | tf_op jit(solution)/shard_map/attention_backward/pallas_call | solution.py:804
  80.0 2.0 %place_results.1 = (bf16[2,16,8192]{2,1,0:T(8,128)(2,1)}, f32[2,16,1024]{2,1,0:T(8,128)}, f32[2,16,1024]{2,1,0:T(8,128)}) custom-call(bf16[2,16,8192]{2,1,0:T(8,128)(2,1)} %get-tuple-element.6.refs_0_, f32[2,16,1024]{2,1,0:T(8,128)} %get-tuple-element.7.refs_1_, f32[2,16,1024]{2,1,0:T(8,128)} %get-tuple-element.8.refs_2_), custom_call_target="tpu_custom_call" | custom-call | tf_op jit(solution)/shard_map/place_results/pallas_call | solution.py:878

commit v5 on v4

--- a/solution.py
+++ b/solution.py
@@ -551,24 +551,49 @@
         for g in range(group):
             dd[s, 0:1, g * bl : (g + 1) * bl] = turn[g : g + 1, :]
 
+    def low_chunk(s, slot, cols, values, scale_at):
+        prob = weights[slot, :, cols] * inverse[scale_at, s, 0:1, cols]
+        d_prob = nt_dot(values, cs[s, cols, :])
+        low_p[s, :, cols] = prob.astype(jnp.bfloat16)
+        low_s[s, :, cols] = (prob * (d_prob - dd[s, 0:1, cols])).astype(jnp.bfloat16)
+
+    def d_value(s):
+        return nn_dot(low_p[s], cs[s])
+
+    def d_key(s):
+        return nn_dot(low_s[s], qs[s])
+
+    def d_query(s):
+        dqt[s] += nn_dot(keys_t[...], low_s[s])
+
     def backward(s, slot, values, scale_at):
         for cols in every:
-            prob = weights[slot, :, cols] * inverse[scale_at, s, 0:1, cols]
-            d_prob = nt_dot(values, cs[s, cols, :])
-            low_p[:, cols] = prob.astype(jnp.bfloat16)
-            low_s[:, cols] = (prob * (d_prob - dd[s, 0:1, cols])).astype(jnp.bfloat16)
-        d_value = nn_dot(low_p[...], cs[s])
-        d_key = nn_dot(low_s[...], qs[s])
-        dqt[s] += nn_dot(keys_t[...], low_s[...])
-        return d_key, d_value
+            low_chunk(s, slot, cols, values, scale_at)
+        made = d_key(s), d_value(s)
+        d_query(s)
+        return made
+
+    def backward_both(t, values, scale_at):
+        for cols in every:
+            low_chunk(1, npair + t, cols, values, scale_at)
+        todo = [d_key, d_value, d_query]
+        made = []
+        for cols in every:
+            low_chunk(0, t, cols, values, scale_at)
+            if todo:
+                made.append(todo.pop(0)(1))
+        for product in todo:
+            made.append(product(1))
+        made = made[0] + d_key(0), made[1] + d_value(0)
+        d_query(0)
+        return made
 
     def turn_keys(keys):
         keys_t[...] = jnp.transpose(keys.astype(jnp.float32)).astype(jnp.bfloat16)
 
-    def put(t, i, value, add):
+    def put(t, i, value):
         for c in range(2):
-            part = value[c * bl : (c + 1) * bl]
-            dkv[t, i, c] = dkv[t, i, c] + part if add else part
+            dkv[t, i, c] = value[c * bl : (c + 1) * bl]
 
     def core_copy(t):
         return remote(
@@ -643,13 +668,15 @@
         q = n + 2
         t = me.pair_of(q)
         turn_keys(doc_kv(0, t))
-        for i, value in enumerate(backward(1, npair + t, doc_kv(1, t), q // 8)):
-            put(t, i, value, False)
+        @pl.when(t > own_pair)
+        def _():
+            for i, value in enumerate(backward(1, npair + t, doc_kv(1, t), q // 8)):
+                put(t, i, value)
 
         @pl.when(t <= own_pair)
         def _():
-            for i, value in enumerate(backward(0, t, doc_kv(1, t), q // 8)):
-                put(t, i, value, True)
+            for i, value in enumerate(backward_both(t, doc_kv(1, t), q // 8)):
+                put(t, i, value)
 
         core_copy(t).start()
 
@@ -826,8 +853,8 @@
             space((3, 2, 1, rows), f32),
             space((2, HD, rows), f32),
             space((HD, 2 * bl), b16),
-            space((2 * bl, rows), b16),
-            space((2 * bl, rows), b16),
+            space((2, 2 * bl, rows), b16),
+            space((2, 2 * bl, rows), b16),
             space((npair, 2, 2, bl, HD), f32),
             space((2, 2 * bl, HD), f32),
             space((2, bl, gw), b16),

time: 82.7 us -> 81.9 us (level)
  no operation moved by 1% of the time
where the time goes in v5:
time: 81.9 us; the launch traced here: 81.3 us
  Pallas kernels  80.6 us (98%)
    pallas_call x1, Pallas kernels, shards(): pl.pallas_call(functools.partial(kernel, dims), out_shape=made, in_specs=...  78.7 us
    pallas_call x1, Pallas kernels, shards(): pl.pallas_call(place_results, out_shape=made, in_specs=[hbm] * 3, out_spe...  1.96 us

profile of v5, /device:TPU:4, one launch (start us, length us, event | category | flops | bytes accessed | tf_op | source)
XLA Modules:
  0.0 81.3 jit_solution(6133407204338162415)
XLA Ops:
  0.6 78.7 %attention_backward.1 = (bf16[2,16,8192]{2,1,0:T(8,128)(2,1)}, f32[2,16,1024]{2,1,0:T(8,128)}, f32[2,16,1024]{2,1,0:T(8,128)}) custom-call(s32[1,256]{1,0:T(1,128)} %bitcast.1, bf16[2,16,8192]{2,1,0:T(8,128)(2,1)} %q_ref.1, bf16[2,16,1024]{2,1,0:T(8,128)(2,1)} %k_ref.1, bf16[2,16,1024]{2,1,0:T(8,128)(2,1)} %v_ref.1, bf16[2,16,8192]{2,1,0:T(8,128)(2,1)} %o_ref.1, ...), custom_call_target="tpu_custom_call" | custom-call | tf_op jit(solution)/shard_map/attention_backward/pallas_call | solution.py:831
  79.3 2.0 %place_results.1 = (bf16[2,16,8192]{2,1,0:T(8,128)(2,1)}, f32[2,16,1024]{2,1,0:T(8,128)}, f32[2,16,1024]{2,1,0:T(8,128)}) custom-call(bf16[2,16,8192]{2,1,0:T(8,128)(2,1)} %get-tuple-element.6.refs_0_, f32[2,16,1024]{2,1,0:T(8,128)} %get-tuple-element.7.refs_1_, f32[2,16,1024]{2,1,0:T(8,128)} %get-tuple-element.8.refs_2_), custom_call_target="tpu_custom_call" | custom-call | tf_op jit(solution)/shard_map/place_results/pallas_call | solution.py:905

commit v6 on v5

--- a/solution.py
+++ b/solution.py
@@ -493,12 +493,13 @@
 
         lax.fori_loop(low, high, step, 0)
 
-    gather_step(1)
+    gather_step(1, (0,))
     for i in range(2):
         locals_[2 * i + 1].wait()
         received_all(kvq.at[i, 1, peer_rows], kv_recv.at[i, 1])
     tail_copy.start()
-    gather_step(2)
+    gather_step(2, (0,))
+    gather_step(1, (1,))
     for copy in own_q:
         copy.wait()
     for kind in range(2):
@@ -512,7 +513,8 @@
     peak_sweep(1, question_kv(0), question_mask, every)
     for f in range(1, me.half - 1):
         if f + 1 > 2:
-            gather_step(f + 1)
+            gather_step(f + 1, (0,))
+            gather_step(f, (1,))
         peaks(f)
     for s in range(2):
         first_max[s] = jnp.max(peak[s], axis=0, keepdims=True)
@@ -521,11 +523,11 @@
     weigh(near, last + 1, first_max)
     if me.half > 2:
         gather_step(me.half, (0,))
+        gather_step(me.half - 1, (1,))
     weigh(8, near, first_max)
-    if me.half > 2:
-        gather_step(me.half, (1,))
     peaks(me.half - 1)
     peaks(me.half)
+    gather_step(me.half, (1,))
     for s in range(2):
         final_max[s] = jnp.max(peak[s], axis=0, keepdims=True)
         total[s] = total[s] * jnp.exp2((first_max[s] - final_max[s]) * EXP2_SCALE)

time: 81.9 us -> 81.1 us (level)
  Pallas kernels: 80.6 us -> 79.7 us
    pallas_call x1, Pallas kernels: 78.7 us -> 77.7 us  [shards(): pl.pallas_call(functools.partial(kernel, dims), out_shape=made, in_specs=...]
where the time goes in v6:
time: 81.1 us; the launch traced here: 80.3 us
  Pallas kernels  79.7 us (98%)
    pallas_call x1, Pallas kernels, shards(): pl.pallas_call(functools.partial(kernel, dims), out_shape=made, in_specs=...  77.7 us
    pallas_call x1, Pallas kernels, shards(): pl.pallas_call(place_results, out_shape=made, in_specs=[hbm] * 3, out_spe...  1.96 us

profile of v6, /device:TPU:4, one launch (start us, length us, event | category | flops | bytes accessed | tf_op | source)
XLA Modules:
  0.0 80.3 jit_solution(18249479189351634643)
XLA Ops:
  0.6 77.7 %attention_backward.1 = (bf16[2,16,8192]{2,1,0:T(8,128)(2,1)}, f32[2,16,1024]{2,1,0:T(8,128)}, f32[2,16,1024]{2,1,0:T(8,128)}) custom-call(s32[1,256]{1,0:T(1,128)} %bitcast.1, bf16[2,16,8192]{2,1,0:T(8,128)(2,1)} %q_ref.1, bf16[2,16,1024]{2,1,0:T(8,128)(2,1)} %k_ref.1, bf16[2,16,1024]{2,1,0:T(8,128)(2,1)} %v_ref.1, bf16[2,16,8192]{2,1,0:T(8,128)(2,1)} %o_ref.1, ...), custom_call_target="tpu_custom_call" | custom-call | tf_op jit(solution)/shard_map/attention_backward/pallas_call | solution.py:833
  78.4 2.0 %place_results.1 = (bf16[2,16,8192]{2,1,0:T(8,128)(2,1)}, f32[2,16,1024]{2,1,0:T(8,128)}, f32[2,16,1024]{2,1,0:T(8,128)}) custom-call(bf16[2,16,8192]{2,1,0:T(8,128)(2,1)} %get-tuple-element.6.refs_0_, f32[2,16,1024]{2,1,0:T(8,128)} %get-tuple-element.7.refs_1_, f32[2,16,1024]{2,1,0:T(8,128)} %get-tuple-element.8.refs_2_), custom_call_target="tpu_custom_call" | custom-call | tf_op jit(solution)/shard_map/place_results/pallas_call | solution.py:907

commit v7 on v6

--- a/solution.py
+++ b/solution.py
@@ -15,7 +15,7 @@
 EXP2_SCALE = SCALE * math.log2(math.e)
 MESH = pl.DeviceIdType.MESH
 LAG = 2
-UNROLL = 4
+UNROLL = 8
 
 
 def remote(src, dst, send_sem, recv_sem, device):

time: 81.1 us -> 81.1 us (level)
  no operation moved by 1% of the time
where the time goes in v7:
time: 81.1 us; the launch traced here: 80.3 us
  Pallas kernels  79.7 us (98%)
    pallas_call x1, Pallas kernels, shards(): pl.pallas_call(functools.partial(kernel, dims), out_shape=made, in_specs=...  77.7 us
    pallas_call x1, Pallas kernels, shards(): pl.pallas_call(place_results, out_shape=made, in_specs=[hbm] * 3, out_spe...  1.96 us

profile of v7, /device:TPU:4, one launch (start us, length us, event | category | flops | bytes accessed | tf_op | source)
XLA Modules:
  0.0 80.3 jit_solution(8558451575372511519)
XLA Ops:
  0.6 77.7 %attention_backward.1 = (bf16[2,16,8192]{2,1,0:T(8,128)(2,1)}, f32[2,16,1024]{2,1,0:T(8,128)}, f32[2,16,1024]{2,1,0:T(8,128)}) custom-call(s32[1,256]{1,0:T(1,128)} %bitcast.1, bf16[2,16,8192]{2,1,0:T(8,128)(2,1)} %q_ref.1, bf16[2,16,1024]{2,1,0:T(8,128)(2,1)} %k_ref.1, bf16[2,16,1024]{2,1,0:T(8,128)(2,1)} %v_ref.1, bf16[2,16,8192]{2,1,0:T(8,128)(2,1)} %o_ref.1, ...), custom_call_target="tpu_custom_call" | custom-call | tf_op jit(solution)/shard_map/attention_backward/pallas_call | solution.py:833
  78.4 2.0 %place_results.1 = (bf16[2,16,8192]{2,1,0:T(8,128)(2,1)}, f32[2,16,1024]{2,1,0:T(8,128)}, f32[2,16,1024]{2,1,0:T(8,128)}) custom-call(bf16[2,16,8192]{2,1,0:T(8,128)(2,1)} %get-tuple-element.6.refs_0_, f32[2,16,1024]{2,1,0:T(8,128)} %get-tuple-element.7.refs_1_, f32[2,16,1024]{2,1,0:T(8,128)} %get-tuple-element.8.refs_2_), custom_call_target="tpu_custom_call" | custom-call | tf_op jit(solution)/shard_map/place_results/pallas_call | solution.py:907
